TPU v7x, 128 devices: a whole 4x4x4 slice. The times are simulated.
128 devices in a mesh: grp: 8 (over y, core), dom: 16 (over z, x).
Axes of the slice: x: 4, y: 4, z: 4, core: 2. Of those that a mesh axis runs over, the one named last changes fastest.
Arguments:
- diag_blocks: bfloat16 [2048, 384, 384], P(('grp', 'dom')), may hold values from -0.3125 to 0.3125
- face_in: bfloat16 [4096, 384, 384], P(('grp', 'dom')), may hold values from -0.3125 to 0.3125
- face_cross: bfloat16 [2048, 384, 384], P(('grp', 'dom')), may hold values from -0.3125 to 0.3125
- metric: float32 [2048, 384], P(('grp', 'dom')), may hold values from 0.5 to 2
- source_in: int32 [4096], P(('grp', 'dom')), may hold values from 0 to 15
- source_cross: int32 [2048], P(('grp', 'dom')), may hold values from 0 to 15
- orient_in: int32 [4096], P(('grp', 'dom')), may hold values from 0 to 7
- orient_cross: int32 [2048], P(('grp', 'dom')), may hold values from 0 to 7
- peer_in: int32 [4096, 1], P(('grp', 'dom')), may hold values from 0 to 15; in each aligned block of 32 rows (0 to 31, 32 to 63, ...) at most 3 rows name the same one
- peer_cross: int32 [2048, 1], P(('grp', 'dom')), may hold values from 0 to 7; in each aligned block of 16 rows (0 to 15, 16 to 31, ...) at most 3 rows name the same one
- target_in: int32 [4096], P(('grp', 'dom')), may hold values from 0 to 47
- target_cross: int32 [2048], P(('grp', 'dom')), may hold values from 0 to 47
Outputs:
- coarse_diag: float32 [2048, 2304], P('grp')
- coarse_face: float32 [2048, 6912], P('grp')
Inputs may be any that keep to these rules, and one draw needn't show every extreme that they name: `peer_in`: at most 3 records of one device name the same partition; on some device exactly 3 do. `peer_cross`: at most 3 records of one device name the same group; on some device exactly 3 do.
All inputs are finite; a program needn't handle non-finite values.
Results may differ from a plain program's by a relative error of at most 0.0052.
Values may be sent and summed in bfloat16 or wider, within the bound.
A program may use at most 128 MiB of HBM per device.

v0:
```python
import jax
import jax.numpy as jnp
from jax import lax
from jax.sharding import PartitionSpec as P


def corner_table(var_count):
    nodes = -1.0 + 2.0 * jnp.arange(4, dtype=jnp.float32) / 3.0
    basis = jnp.stack(((1.0 - nodes) / 2.0, (1.0 + nodes) / 2.0), axis=1)
    cube = jnp.einsum("ia,jb,kc->abcijk", basis, basis, basis).reshape(8, 64)
    return jnp.kron(jnp.eye(var_count, dtype=jnp.float32), cube)


def restrictor(weights, orient):
    var_count = weights.shape[1] // 64
    table = corner_table(var_count)
    full = weights[:, None, :] * table[None]
    shaped = full.reshape(weights.shape[0], var_count * 8, var_count, 4, 4, 4)
    bits = orient.reshape(-1, 1, 1, 1, 1, 1)
    shaped = jnp.where(bits % 2 == 1, jnp.flip(shaped, 3), shaped)
    shaped = jnp.where(bits // 2 % 2 == 1, jnp.flip(shaped, 4), shaped)
    shaped = jnp.where(bits // 4 % 2 == 1, jnp.flip(shaped, 5), shaped)
    return shaped.reshape(weights.shape[0], var_count * 8, var_count * 64).astype(jnp.bfloat16)


def pick_rows(index, table):
    picks = (index[:, None] == jnp.arange(table.shape[0], dtype=jnp.int32)[None, :]).astype(
        jnp.float32
    )
    return jnp.dot(picks, table, precision=lax.Precision.HIGHEST)


def place_rows(targets, values, row_count):
    picks = (jnp.arange(row_count, dtype=jnp.int32)[:, None] == targets[None, :]).astype(
        jnp.float32
    )
    return jnp.dot(picks, values, precision=lax.Precision.HIGHEST)


def one_sided(blocks, column_side):
    return jnp.einsum(
        "rcj,rij->rci", column_side, blocks, preferred_element_type=jnp.float32
    ).astype(jnp.bfloat16)


def coarse_terms(row_side, products):
    return jnp.einsum("rci,rdi->rcd", row_side, products, preferred_element_type=jnp.float32)


def pack_records(products, targets, peers, peer_count, capacity):
    count = products.shape[0]
    onehot = (peers[:, None] == jnp.arange(peer_count, dtype=jnp.int32)[None, :]).astype(jnp.int32)
    order_rank = jnp.sum((jnp.cumsum(onehot, axis=0) - 1) * onehot, axis=1)
    position = peers * capacity + order_rank
    places = jnp.arange(peer_count * capacity, dtype=jnp.int32)
    picks = places[:, None] == position[None, :]
    flattened = products.reshape(count, -1)
    packed = jnp.dot(
        picks.astype(jnp.bfloat16), flattened, preferred_element_type=jnp.float32
    ).astype(jnp.bfloat16)
    slot_ids = jnp.sum(jnp.where(picks, targets[None, :] + 1, 0), axis=1) - 1
    return (
        packed.reshape((peer_count, capacity) + products.shape[1:]),
        slot_ids.reshape(peer_count, capacity),
    )


def per_device(
    diag_blocks,
    face_in,
    face_cross,
    metric,
    source_in,
    source_cross,
    orient_in,
    orient_cross,
    peer_in,
    peer_cross,
    target_in,
    target_cross,
):
    elem_count = metric.shape[0]
    coarse_width = metric.shape[1] // 8
    square = coarse_width * coarse_width
    group_width = lax.axis_size("dom")
    group_count = lax.axis_size("grp")
    cross_capacity = (face_cross.shape[0] + group_count - 1) // group_count + 1
    inner_capacity = (face_in.shape[0] + group_width - 1) // group_width + 1

    def receive(packet):
        products, slot_ids = packet
        peers_here, items = slot_ids.shape
        flat_ids = slot_ids.reshape(-1)
        row_side = restrictor(
            pick_rows(flat_ids // 3, metric), jnp.zeros(flat_ids.shape, jnp.int32)
        )
        terms = coarse_terms(
            row_side, products.reshape(peers_here * items, products.shape[2], products.shape[3])
        )
        return (terms.reshape(peers_here, items, square), slot_ids)

    diag_side = restrictor(metric, jnp.zeros((elem_count,), jnp.int32))
    diag_coarse = coarse_terms(diag_side, one_sided(diag_blocks, diag_side)).reshape(
        elem_count, square
    )
    cross_side = restrictor(pick_rows(source_cross, metric), orient_cross)
    cross_products = one_sided(face_cross, cross_side)
    inner_side = restrictor(pick_rows(source_in, metric), orient_in)
    inner_products = one_sided(face_in, inner_side)
    cross_packed, cross_ids = pack_records(
        cross_products, target_cross, peer_cross[:, 0], group_count, cross_capacity
    )
    cross_terms, cross_got = receive(
        (
            lax.all_to_all(cross_packed, "grp", split_axis=0, concat_axis=0, tiled=True),
            lax.all_to_all(cross_ids, "grp", split_axis=0, concat_axis=0, tiled=True),
        )
    )
    inner_packed, inner_ids = pack_records(
        inner_products, target_in, peer_in[:, 0], group_width, inner_capacity
    )
    inner_terms, inner_got = receive(
        (
            lax.all_to_all(inner_packed, "dom", split_axis=0, concat_axis=0, tiled=True),
            lax.all_to_all(inner_ids, "dom", split_axis=0, concat_axis=0, tiled=True),
        )
    )
    face_local = place_rows(cross_got.reshape(-1), cross_terms.reshape(-1, square), 3 * elem_count)
    face_local = face_local + place_rows(
        inner_got.reshape(-1), inner_terms.reshape(-1, square), 3 * elem_count
    )
    face_local = face_local.reshape(elem_count, 3 * square)
    coarse_diag, coarse_face = (
        lax.all_gather(diag_coarse, "dom", axis=0, tiled=True),
        lax.all_gather(face_local, "dom", axis=0, tiled=True),
    )
    return (coarse_diag, coarse_face)


def solution(mesh):
    placed = (
        P(("grp", "dom"), None, None),
        P(("grp", "dom"), None, None),
        P(("grp", "dom"), None, None),
        P(("grp", "dom"), None),
        P(("grp", "dom")),
        P(("grp", "dom")),
        P(("grp", "dom")),
        P(("grp", "dom")),
        P(("grp", "dom"), None),
        P(("grp", "dom"), None),
        P(("grp", "dom")),
        P(("grp", "dom")),
    )
    return jax.shard_map(
        per_device,
        mesh=mesh,
        in_specs=placed,
        out_specs=(P("grp", None), P("grp", None)),
        check_vma=False,
    )
```

profile of v0, /device:TPU:1, one launch (start us, length us, event | category | flops | bytes accessed | tf_op | source)
XLA Modules:
  0.0 180.3 jit_solution(1263921991991287014)
XLA Ops:
  7.2 0.7 fusion.33
  7.9 0.8 select_reduce_fusion.3
  8.8 0.7 multiply_add_fusion.1
  9.5 0.7 sub.80
  10.2 6.0 %all-to-all-start = ((s32[8,1,3]{2,1,0:T(1,128)}), s32[8,1,3]{2,1,0:T(1,128)S(1)}, u32[]{:S(2)}, u32[]{:S(2)}) async-start(s32[8,1,3]{2,1,0:T(1,128)} %bitcast.3), calls=%async_computation | async-start | bytes 8192 | tf_op jit(solution)/shard_map/all_to_all | solution.py:116
  17.0 4.3 %fusion.15 = f32[16,48,48]{2,1,0:T(8,128)S(1)} fusion(bf16[16,384,384]{2,1,0:T(8,128)(2,1)} %param.12, f32[48,384]{1,0:T(8,128)S(1)} %copy.40, f32[16,384]{1,0:T(8,128)} %param.15), kind=kOutput, calls=%fused_computation.25 | convolution fusion | flops 256278528 | bytes 4964352 | tf_op jit(solution)/shard_map/rci,rdi->rcd/dot_general | solution.py:47
  21.4 0.8 reshape.407
  22.3 0.4 fusion.34
  22.6 1.0 broadcast_multiply_fusion.1
  23.7 0.6 reverse_select_fusion.5
  24.3 0.7 reverse_select_fusion.4
  25.0 0.8 fusion.1
  25.9 1.8 fusion.12
  27.6 0.9 copy.51
  28.6 0.4 fusion.26
  29.0 1.9 %broadcast_multiply_fusion = bf16[32,48,6,4,4,4]{1,0,5,4,3,2:T(8,128)(2,1)S(1)} fusion(f32[48,6,4,4,4]{0,4,3,2,1:T(4,128)S(1)} %broadcast_multiply_fusion.2, f32[32,6,4,4,4]{0,4,3,2,1:T(4,128)S(1)} %bitcast.55), kind=kLoop, calls=%fused_computation.14 | loop fusion | flops 1179648 | bytes 1302528 | tf_op jit(solution)/shard_map/mul | solution.py:17
  31.1 0.2 select_reduce_fusion.1
  31.3 1.0 reverse_select_fusion.2
  32.5 1.5 reverse_select_fusion.1
  34.0 1.1 fusion
  35.1 0.7 sub.86
  35.8 7.6 %all-to-all-start.2 = ((s32[16,1,3]{2,1,0:T(1,128)}), s32[16,1,3]{2,1,0:T(1,128)S(1)}, u32[]{:S(2)}, u32[]{:S(2)}) async-start(s32[16,1,3]{2,1,0:T(1,128)} %bitcast.8), calls=%async_computation.2 | async-start | bytes 16384 | tf_op jit(solution)/shard_map/all_to_all | solution.py:125
  43.4 1.6 convolution_convert_fusion.1
  45.0 1.0 copy.52
  46.0 3.8 %all-to-all-done.2 = s32[16,1,3]{2,1,0:T(1,128)S(1)} async-done(((s32[16,1,3]{2,1,0:T(1,128)}), s32[16,1,3]{2,1,0:T(1,128)S(1)}, u32[]{:S(2)}, u32[]{:S(2)}) %all-to-all-start.2) | async-done | bytes 224 | tf_op jit(solution)/shard_map/all_to_all | solution.py:125
  49.9 6.1 %all-to-all-start.1 = ((bf16[8,3,48,384]{3,2,1,0:T(8,128)(2,1)}), bf16[8,3,48,384]{3,2,1,0:T(8,128)(2,1)}, u32[]{:S(2)}, u32[]{:S(2)}) async-start(bf16[8,3,48,384]{3,2,1,0:T(8,128)(2,1)} %bitcast.49), calls=%async_computation.1 | async-start | bytes 1769472 | tf_op jit(solution)/shard_map/all_to_all | solution.py:115
  55.9 7.7 %fusion.9 = bf16[32,48,384]{2,1,0:T(8,128)(2,1)S(1)} fusion(bf16[32,384,384]{2,1,0:T(8,128)(2,1)} %param.13, bf16[32,48,384]{1,0,2:T(8,128)(2,1)S(1)} %bitcast.42), kind=kOutput, calls=%fused_computation.22 | convolution fusion | flops 453574656 | bytes 11796480 | tf_op jit(solution)/shard_map/rcj,rij->rci/dot_general | solution.py:41
  63.7 0.3 copy.53
  63.9 0.7 convolution_convert_fusion
  64.7 1.4 copy.54
  66.1 3.1 %all-to-all-done.1 = bf16[8,3,48,384]{3,2,1,0:T(8,128)(2,1)} async-done(((bf16[8,3,48,384]{3,2,1,0:T(8,128)(2,1)}), bf16[8,3,48,384]{3,2,1,0:T(8,128)(2,1)}, u32[]{:S(2)}, u32[]{:S(2)}) %all-to-all-start.1) | async-done | bytes 884768 | tf_op jit(solution)/shard_map/all_to_all | solution.py:115
  69.3 3.7 %all-to-all-start.3 = ((bf16[16,3,48,384]{3,2,1,0:T(8,128)(2,1)}), bf16[16,3,48,384]{3,2,1,0:T(8,128)(2,1)S(1)}, u32[]{:S(2)}, u32[]{:S(2)}) async-start(bf16[16,3,48,384]{3,2,1,0:T(8,128)(2,1)} %bitcast.23), calls=%async_computation.3 | async-start | bytes 3538944 | tf_op jit(solution)/shard_map/all_to_all | solution.py:124
  73.0 0.5 broadcast.910
  73.5 0.7 reduce.6
  74.3 0.2 fusion.30
  74.5 0.7 reduce.7
  75.3 0.2 fusion.24
  75.5 1.6 fusion.16
  77.1 0.3 reshape_reshape.6
  77.4 0.3 fusion.23
  77.7 21.1 %all-to-all-done.3 = bf16[16,3,48,384]{3,2,1,0:T(8,128)(2,1)S(1)} async-done(((bf16[16,3,48,384]{3,2,1,0:T(8,128)(2,1)}), bf16[16,3,48,384]{3,2,1,0:T(8,128)(2,1)S(1)}, u32[]{:S(2)}, u32[]{:S(2)}) %all-to-all-start.3) | async-done | bytes 1769504 | tf_op jit(solution)/shard_map/all_to_all | solution.py:124
  98.9 0.7 fusion.4
  99.6 0.5 reshape_reshape.7
  100.2 0.3 convolution_add_fusion
  100.5 0.9 reshape.414
  101.4 62.3 %all-gather.5.cloned.1.call-done = f32[256,6912]{1,0:T(8,128)} async-done(((f32[16,6912]{1,0:T(8,128)}), f32[256,6912]{1,0:T(8,128)}) %all-gather.5.cloned.1.call-update) | async-done | bytes 7077904 | tf_op jit(solution)/shard_map/all_gather | solution.py:135
  163.8 3.2 %copy.65 = f32[256,2304]{1,0:T(8,128)} copy(f32[256,2304]{1,0:T(8,128)} %all-gather.3.cloned.1.call-done) | data formatting | bytes 4718592
  167.0 6.4 %copy.66 = f32[256,6912]{1,0:T(8,128)} copy(f32[256,6912]{1,0:T(8,128)} %all-gather.5.cloned.1.call-done) | data formatting | bytes 14155776
  (52 shorter events, 1.6 us)
Async XLA Ops:
  10.2 25.6 %all-to-all-start = ((s32[8,1,3]{2,1,0:T(1,128)}), s32[8,1,3]{2,1,0:T(1,128)S(1)}, u32[]{:S(2)}, u32[]{:S(2)}) async-start(s32[8,1,3]{2,1,0:T(1,128)} %bitcast.3), calls=%async_computation | async-start | bytes 8192 | tf_op jit(solution)/shard_map/all_to_all | solution.py:116
  16.2 85.3 %all-gather.3.cloned.1.call-start = ((), (), s32[]{:S(2)}) async-start(), calls=%async_computation.4 | async-start | bytes 2506752 | tf_op jit(solution)/shard_map/all_gather | solution.py:134
  17.0 5.2 %copy-start = (f32[16,384]{1,0:T(8,128)S(1)}, f32[16,384]{1,0:T(8,128)}, u32[]{:S(2)}) copy-start(f32[16,384]{1,0:T(8,128)} %param.15) | copy-start | bytes 73732
  17.0 5.2 %copy-start.2 = (s32[16]{0:T(128)S(1)}, s32[16]{0:T(128)}, u32[]{:S(2)}) copy-start(s32[16]{0:T(128)} %param.17) | copy-start | bytes 196
  17.0 8.7 %slice-start = ((s8[4718592]{0:T(1024)(128)(4,1)}), s8[524288]{0:T(1024)(128)(4,1)S(1)}, s32[]{:S(2)}) async-start(s8[4718592]{0:T(1024)(128)(4,1)} %bitcast.46), calls=%async_computation.6 | async-start | bytes 1048576
  21.4 2.3 %copy-start.5 = (s32[16]{0:T(128)S(1)}, s32[16]{0:T(128)}, u32[]{:S(2)}) copy-start(s32[16]{0:T(128)} %param.19) | copy-start | bytes 196
  23.7 2.2 %slice-start.1 = ((s8[4718592]{0:T(1024)(128)(4,1)}), s8[4194304]{0:T(1024)(128)(4,1)S(1)}, s32[]{:S(2)}) async-start(s8[4718592]{0:T(1024)(128)(4,1)} %bitcast.46), calls=%async_computation.7 | async-start | bytes 8388608
  25.9 2.7 %copy-start.3 = (s32[32]{0:T(128)S(1)}, s32[32]{0:T(128)}, u32[]{:S(2)}) copy-start(s32[32]{0:T(128)} %param.16) | copy-start | bytes 388
  29.0 2.0 %copy-start.6 = (s32[32]{0:T(128)S(1)}, s32[32]{0:T(128)}, u32[]{:S(2)}) copy-start(s32[32]{0:T(128)} %param.18) | copy-start | bytes 388
  29.0 2.0 %copy-start.1 = (s32[32,1]{0,1:T(1,128)S(1)}, s32[32,1]{0,1:T(1,128)}, u32[]{:S(2)}) copy-start(s32[32,1]{0,1:T(1,128)} %param.20) | copy-start | bytes 388
  31.3 1.1 copy-start.4
  35.8 14.0 %all-to-all-start.2 = ((s32[16,1,3]{2,1,0:T(1,128)}), s32[16,1,3]{2,1,0:T(1,128)S(1)}, u32[]{:S(2)}, u32[]{:S(2)}) async-start(s32[16,1,3]{2,1,0:T(1,128)} %bitcast.8), calls=%async_computation.2 | async-start | bytes 16384 | tf_op jit(solution)/shard_map/all_to_all | solution.py:125
  49.9 19.4 %all-to-all-start.1 = ((bf16[8,3,48,384]{3,2,1,0:T(8,128)(2,1)}), bf16[8,3,48,384]{3,2,1,0:T(8,128)(2,1)}, u32[]{:S(2)}, u32[]{:S(2)}) async-start(bf16[8,3,48,384]{3,2,1,0:T(8,128)(2,1)} %bitcast.49), calls=%async_computation.1 | async-start | bytes 1769472 | tf_op jit(solution)/shard_map/all_to_all | solution.py:115
  69.3 29.6 %all-to-all-start.3 = ((bf16[16,3,48,384]{3,2,1,0:T(8,128)(2,1)}), bf16[16,3,48,384]{3,2,1,0:T(8,128)(2,1)S(1)}, u32[]{:S(2)}, u32[]{:S(2)}) async-start(bf16[16,3,48,384]{3,2,1,0:T(8,128)(2,1)} %bitcast.23), calls=%async_computation.3 | async-start | bytes 3538944 | tf_op jit(solution)/shard_map/all_to_all | solution.py:124
  73.0 90.8 %all-gather.5.cloned.1.call-start = ((), (), s32[]{:S(2)}) async-start(), calls=%async_computation.5 | async-start | bytes 7520256 | tf_op jit(solution)/shard_map/all_gather | solution.py:135
Sparse Core Ops, SparseCore 0:
  22.4 46.2 all-gather.2
  101.5 62.1 all-gather.4
where the time goes:
time: 181 us; the launch traced here: 180 us
  waiting for transfers between devices  90.5 us (50%)
  starting transfers between devices  23.4 us (13%)
  matrix products  20.3 us (11%)
  local copies, waits for them, and re-layouts  18.6 us (10%)
  between operations  14.4 us (8%)
  other arithmetic  13.1 us (7%)
    all_gather x1, waiting for transfers between devices, per_device(): lax.all_gather(face_local, 'dom', axis=0, tiled=True)  62.3 us
    all_to_all x1, waiting for transfers between devices, per_device(): lax.all_to_all(inner_packed, 'dom', split_axis=0, concat_axis=0, tiled=True)  21.1 us
    unnamed x24, local copies, waits for them, and re-layouts  13.4 us
    dot_general x2, matrix products, one_sided(): jnp.einsum('rcj,rij->rci', column_side, blocks, preferred_element_type=jn...  9.53 us
    all_to_all x1, starting transfers between devices, per_device(): lax.all_to_all(inner_ids, 'dom', split_axis=0, concat_axis=0, tiled=True)  7.6 us
    dot_general x3, matrix products, coarse_terms(): jnp.einsum('rci,rdi->rcd', row_side, products, preferred_element_type=jnp...  6.65 us
    all_to_all x1, starting transfers between devices, per_device(): lax.all_to_all(cross_packed, 'grp', split_axis=0, concat_axis=0, tiled=True)  6.07 us
    all_to_all x1, starting transfers between devices, per_device(): lax.all_to_all(cross_ids, 'grp', split_axis=0, concat_axis=0, tiled=True)  5.96 us
  transfers between devices with their start and end apart: 6, of which 4 were waited for; matrix products, arithmetic and copies ran while one was open for 22% of the time, Pallas kernels for 0%

commit v1 on v0

v1 whole, which is shorter than its diff:
```python
import jax
import jax.numpy as jnp
from jax import lax
from jax.sharding import PartitionSpec as P

CROSS_CAP = 3


def corner_table(var_count):
    nodes = -1.0 + 2.0 * jnp.arange(4, dtype=jnp.float32) / 3.0
    basis = jnp.stack(((1.0 - nodes) / 2.0, (1.0 + nodes) / 2.0), axis=1)
    cube = jnp.einsum("ia,jb,kc->abcijk", basis, basis, basis).reshape(8, 64)
    return jnp.kron(jnp.eye(var_count, dtype=jnp.float32), cube)


def restrictor(weights, orient):
    var_count = weights.shape[1] // 64
    table = corner_table(var_count)
    full = weights[:, None, :] * table[None]
    shaped = full.reshape(weights.shape[0], var_count * 8, var_count, 4, 4, 4)
    bits = orient.reshape(-1, 1, 1, 1, 1, 1)
    shaped = jnp.where(bits % 2 == 1, jnp.flip(shaped, 3), shaped)
    shaped = jnp.where(bits // 2 % 2 == 1, jnp.flip(shaped, 4), shaped)
    shaped = jnp.where(bits // 4 % 2 == 1, jnp.flip(shaped, 5), shaped)
    return shaped.reshape(weights.shape[0], var_count * 8, var_count * 64).astype(jnp.bfloat16)


def plain_restrictor(weights):
    table = corner_table(weights.shape[1] // 64)
    return (weights[:, None, :] * table[None]).astype(jnp.bfloat16)


def pick_rows(index, table):
    picks = (index[:, None] == jnp.arange(table.shape[0], dtype=jnp.int32)[None, :]).astype(
        jnp.float32
    )
    return jnp.dot(picks, table, precision=lax.Precision.HIGHEST)


def one_sided(blocks, column_side):
    return jnp.einsum(
        "rcj,rij->rci", column_side, blocks, preferred_element_type=jnp.float32
    ).astype(jnp.bfloat16)


def coarse_terms(row_side, products):
    return jnp.einsum("rci,rdi->rcd", row_side, products, preferred_element_type=jnp.float32)


def id_row(values, width):
    flat = values.reshape(-1).astype(jnp.bfloat16)
    return jnp.pad(flat, (0, width - flat.shape[0]))[None, :]


def per_device(
    diag_blocks,
    face_in,
    face_cross,
    metric,
    source_in,
    source_cross,
    orient_in,
    orient_cross,
    peer_in,
    peer_cross,
    target_in,
    target_cross,
):
    elem_count = metric.shape[0]
    coarse_width = metric.shape[1] // 8
    square = coarse_width * coarse_width
    slots_dev = 3 * elem_count
    group_width = lax.axis_size("dom")
    group_count = lax.axis_size("grp")
    my_dom = lax.axis_index("dom")
    my_grp = lax.axis_index("grp")
    inner_count = face_in.shape[0]
    cross_count = face_cross.shape[0]

    metric_dom = lax.all_gather(metric, "dom", axis=0, tiled=True)
    metric_grp = lax.all_gather(metric, "grp", axis=0, tiled=True)

    diag_side = plain_restrictor(metric)
    diag_c = coarse_terms(diag_side, one_sided(diag_blocks, diag_side))
    diag_rows = diag_c.reshape(elem_count, square).astype(jnp.bfloat16)
    diag_all = lax.all_gather(diag_rows, "dom", axis=0, tiled=True)

    cross_y = one_sided(face_cross, restrictor(pick_rows(source_cross, metric), orient_cross))
    peer_x = peer_cross[:, 0]
    cross_row_side = plain_restrictor(
        pick_rows(peer_x * elem_count + target_cross // 3, metric_grp)
    )
    cross_c = coarse_terms(cross_row_side, cross_y).reshape(cross_count, square)
    cross_ids = jnp.stack((peer_x, target_cross), axis=1)
    cross_packet = jnp.concatenate(
        (cross_c.astype(jnp.bfloat16), id_row(cross_ids, square)), axis=0
    )
    cross_got = lax.all_gather(cross_packet, "grp", axis=0)
    got_rows = cross_got[:, :cross_count, :]
    got_ids = cross_got[:, cross_count, : 2 * cross_count].astype(jnp.int32)
    got_peer = got_ids[:, 0::2]
    got_target = got_ids[:, 1::2]
    match = got_peer == my_grp
    rank = jnp.cumsum(match.astype(jnp.int32), axis=1) - 1
    picks = match[:, None, :] & (
        rank[:, None, :] == jnp.arange(CROSS_CAP, dtype=jnp.int32)[None, :, None]
    )
    mine_rows = jnp.einsum(
        "skr,srq->skq", picks.astype(jnp.bfloat16), got_rows, preferred_element_type=jnp.float32
    ).astype(jnp.bfloat16).reshape(group_count * CROSS_CAP, square)
    mine_target = jnp.sum(jnp.where(picks, got_target[:, None, :], 0), axis=2)
    mine_slot = jnp.where(
        jnp.any(picks, axis=2), my_dom * slots_dev + mine_target, -1
    ).reshape(-1)

    inner_y = one_sided(face_in, restrictor(pick_rows(source_in, metric), orient_in))
    peer_i = peer_in[:, 0]
    inner_row_side = plain_restrictor(
        pick_rows(peer_i * elem_count + target_in // 3, metric_dom)
    )
    inner_c = coarse_terms(inner_row_side, inner_y).reshape(inner_count, square)
    inner_slot = peer_i * slots_dev + target_in

    slots = jnp.concatenate((inner_slot, mine_slot), axis=0)
    valid = slots >= 0
    slot_code = jnp.stack(
        (jnp.where(valid, slots // 32, -1), jnp.where(valid, slots % 32, 0)), axis=1
    )
    face_packet = jnp.concatenate(
        (inner_c.astype(jnp.bfloat16), mine_rows, id_row(slot_code, square)), axis=0
    )
    face_all = lax.all_gather(face_packet, "dom", axis=0)
    contrib_count = slots.shape[0]
    contrib = face_all[:, :contrib_count, :].reshape(group_width * contrib_count, square)
    codes = face_all[:, contrib_count, : 2 * contrib_count].astype(jnp.int32)
    hi = codes[:, 0::2].reshape(-1)
    lo = codes[:, 1::2].reshape(-1)
    got_slot = jnp.where(hi >= 0, hi * 32 + lo, -1)
    group_slots = group_width * slots_dev
    onehot = (
        jnp.arange(group_slots, dtype=jnp.int32)[:, None] == got_slot[None, :]
    ).astype(jnp.bfloat16)
    face = jnp.dot(onehot, contrib, preferred_element_type=jnp.float32)

    coarse_diag = diag_all.astype(jnp.float32)
    coarse_face = face.reshape(group_width * elem_count, 3 * square)
    return (coarse_diag, coarse_face)


def solution(mesh):
    placed = (
        P(("grp", "dom"), None, None),
        P(("grp", "dom"), None, None),
        P(("grp", "dom"), None, None),
        P(("grp", "dom"), None),
        P(("grp", "dom")),
        P(("grp", "dom")),
        P(("grp", "dom")),
        P(("grp", "dom")),
        P(("grp", "dom"), None),
        P(("grp", "dom"), None),
        P(("grp", "dom")),
        P(("grp", "dom")),
    )
    return jax.shard_map(
        per_device,
        mesh=mesh,
        in_specs=placed,
        out_specs=(P("grp", None), P("grp", None)),
        check_vma=False,
    )
```

time: 181 us -> 172 us (0.950)
  blocking collectives: 0 us -> 48.4 us
  waiting for transfers between devices: 90.5 us -> 54.5 us
  starting transfers between devices: 23.4 us -> 0.08 us
  matrix products: 20.3 us -> 24.8 us
  local copies, waits for them, and re-layouts: 18.6 us -> 15.2 us
    all_gather x0 -> x3, blocking collectives: none -> 48.4 us  [the longest x1 20.3 us: per_device(): metric_dom = lax.all_gather(metric, 'dom', axis=0, tiled=True)]
    all_to_all x4 -> x0, waiting for transfers between devices: 28.1 us -> none  [the longest x1 21.1 us: per_device(): lax.all_to_all(inner_packed, 'dom', split_axis=0, concat_axis=0, tiled=True)]
    all_to_all x4 -> x0, starting transfers between devices: 23.3 us -> none  [the longest x1 7.6 us: per_device(): lax.all_to_all(inner_ids, 'dom', split_axis=0, concat_axis=0, tiled=True)]
    unnamed x24 -> x18, local copies, waits for them, and re-layouts: 13.4 us -> 0.05 us
    dot_general x3, matrix products: 6.65 us -> 17.4 us  [coarse_terms(): jnp.einsum('rci,rdi->rcd', row_side, products, preferred_element_type=jnp...]
    all_gather x2, waiting for transfers between devices: 62.4 us -> 54.5 us  [the longest x1 54.4 us: per_device(): face_all = lax.all_gather(face_packet, 'dom', axis=0)]
    reshape x2, local copies, waits for them, and re-layouts: 1.74 us -> 8.73 us  [the longest x1 8.64 us: per_device(): coarse_face = face.reshape(group_width * elem_count, 3 * square)]
    dot_general x6 -> x2, matrix products: 12.5 us -> 6.19 us  [the longest x1 5.97 us: per_device(): face = jnp.dot(onehot, contrib, preferred_element_type=jnp.float32)]
  transfers between devices with their start and end apart: 6 -> 2, of which waited for: 4 -> 1; matrix products, arithmetic and copies ran while one was open for 22% -> 18% of each run, Pallas kernels for 0% -> 0%
where the time goes in v1:
time: 172 us
  waiting for transfers between devices  54.5 us (32%)
  blocking collectives  48.4 us (28%)
  matrix products  24.8 us (14%)
  local copies, waits for them, and re-layouts  15.2 us (9%)
  between operations  14.4 us (8%)
  other arithmetic  14.3 us (8%)
    all_gather x1, waiting for transfers between devices, per_device(): face_all = lax.all_gather(face_packet, 'dom', axis=0)  54.4 us
    all_gather x1, blocking collectives, per_device(): metric_dom = lax.all_gather(metric, 'dom', axis=0, tiled=True)  20.3 us
    dot_general x3, matrix products, coarse_terms(): jnp.einsum('rci,rdi->rcd', row_side, products, preferred_element_type=jnp...  17.4 us
    all_gather x1, blocking collectives, per_device(): metric_grp = lax.all_gather(metric, 'grp', axis=0, tiled=True)  14.6 us
    all_gather x1, blocking collectives, per_device(): cross_got = lax.all_gather(cross_packet, 'grp', axis=0)  13.5 us
    reshape x1, local copies, waits for them, and re-layouts, per_device(): coarse_face = face.reshape(group_width * elem_count, 3 * square)  8.64 us
    dot_general x1, matrix products, per_device(): face = jnp.dot(onehot, contrib, preferred_element_type=jnp.float32)  5.97 us
  transfers between devices with their start and end apart: 2, of which 1 were waited for; matrix products, arithmetic and copies ran while one was open for 18% of the time, Pallas kernels for 0%

profile of v1, /device:TPU:1, one launch (start us, length us, event | category | flops | bytes accessed | tf_op | source)
XLA Modules:
  0.0 171.8 jit_solution(11630039760645675383)
XLA Ops:
  7.4 0.1 mul.188
  7.5 0.1 broadcast_multiply_fusion.3
  7.6 0.1 mul.191
  7.8 4.3 %fusion.26 = bf16[16,48,48]{2,1,0:T(8,128)(2,1)S(1)} fusion(bf16[16,384,384]{2,1,0:T(8,128)(2,1)} %param.12, f32[48,384]{1,0:T(8,128)S(1)} %mul.191, f32[16,384]{1,0:T(8,128)} %param.15), kind=kOutput, calls=%fused_computation.30 | convolution fusion | flops 256315392 | bytes 4890624 | tf_op jit(solution)/shard_map/rci,rdi->rcd/dot_general | solution.py:47
  12.0 0.9 convert_element_type.104
  13.1 0.1 copy.31
  13.2 14.6 %all_gather.23 = f32[128,384]{1,0:T(8,128)S(1)} all-gather(f32[16,384]{1,0:T(8,128)S(1)} %copy-done), channel_id=1, replica_groups=mesh['grp'=8,'dom'=16] {'grp'}, dimensions={0}, use_global_device_ids=true | all-gather | bytes 221184 | tf_op jit(solution)/shard_map/all_gather | solution.py:81
  27.8 0.1 mul.206
  28.1 0.4 fusion.43
  28.6 1.0 broadcast_multiply_fusion.1
  29.6 0.6 reverse_select_fusion.5
  30.2 0.7 reverse_select_fusion.4
  30.9 0.7 fusion.1
  31.6 0.2 fusion.42
  31.8 4.3 %fusion.27 = bf16[16,48,48]{2,1,0:T(8,128)(2,1)S(1)} fusion(bf16[16,384,384]{2,1,0:T(8,128)(2,1)} %param.14, bf16[16,48,384]{1,0,2:T(8,128)(2,1)S(1)} %bitcast.38, f32[16,384]{1,0:T(8,128)S(1)} %fusion.42, f32[48,384]{1,0:T(8,128)S(1)} %mul.191), kind=kOutput, calls=%fused_computation.31 | convolution fusion | flops 255725568 | bytes 5480448 | tf_op jit(solution)/shard_map/rci,rdi->rcd/dot_general | solution.py:47
  36.1 0.2 convert_element_type.117
  36.3 0.1 copy.36
  36.4 0.1 convert_element_type.118
  36.6 13.5 %all-gather.2 = bf16[8,17,2304]{2,1,0:T(8,128)(2,1)S(1)} all-gather(bf16[1,17,2304]{2,1,0:T(8,128)(2,1)S(1)} %maximum_bitcast_fusion.1), channel_id=2, replica_groups=mesh['grp'=8,'dom'=16] {'grp'}, dimensions={0}, use_global_device_ids=true | all-gather | bytes 705024 | tf_op jit(solution)/shard_map/all_gather | solution.py:98
  50.1 0.1 slice.25
  50.2 0.1 slice.27
  50.3 0.2 reduce_window_sum.11
  50.5 0.2 fusion.60
  50.7 0.2 convolution_convert_fusion
  50.9 20.3 %all_gather.22 = f32[256,384]{1,0:T(8,128)S(1)} all-gather(f32[16,384]{1,0:T(8,128)S(1)} %copy-done), channel_id=1, replica_groups=mesh['grp'=8,'dom'=16] {'dom'}, dimensions={0}, use_global_device_ids=true | all-gather | bytes 417792 | tf_op jit(solution)/shard_map/all_gather | solution.py:80
  71.2 0.2 select_reduce_fusion
  71.5 0.1 fusion.47
  71.6 0.1 copy.37
  71.7 0.1 convert_element_type.123
  71.9 0.1 reshape.525
  72.0 0.4 fusion.39
  72.4 1.9 %broadcast_multiply_fusion = bf16[32,48,6,4,4,4]{1,0,5,4,3,2:T(8,128)(2,1)S(1)} fusion(f32[48,6,4,4,4]{0,4,3,2,1:T(4,128)S(1)} %broadcast_multiply_fusion.2, f32[32,6,4,4,4]{0,4,3,2,1:T(4,128)S(1)} %bitcast.40), kind=kLoop, calls=%fused_computation.11 | loop fusion | flops 1179648 | bytes 1302528 | tf_op jit(solution)/shard_map/mul | solution.py:19
  74.4 0.3 fusion.37
  74.7 1.3 reverse_select_fusion.2
  76.0 1.5 reverse_select_fusion.1
  77.5 1.1 fusion
  78.6 8.9 %fusion.17 = bf16[32,48,48]{2,1,0:T(8,128)(2,1)} fusion(bf16[32,384,384]{2,1,0:T(8,128)(2,1)} %param.13, bf16[32,48,384]{1,0,2:T(8,128)(2,1)S(1)} %bitcast.37, f32[48,384]{1,0:T(8,128)S(1)} %mul.191, f32[32,384]{1,0:T(8,128)S(1)} %fusion.37), kind=kOutput, calls=%fused_computation.23 | convolution fusion | flops 511451136 | bytes 10887168 | tf_op jit(solution)/shard_map/rci,rdi->rcd/dot_general | solution.py:47
  87.5 1.4 convert_element_type.111
  88.9 0.7 maximum_bitcast_fusion
  89.7 2.8 %convert_element_type.105 = f32[256,2304]{1,0:T(8,128)} convert(bf16[256,2304]{1,0:T(8,128)(2,1)} %all-gather.7.cloned.1.call-done) | non-fusion elementwise | flops 589824 | bytes 3538944 | tf_op jit(solution)/shard_map/convert_element_type | solution.py:145
  92.5 54.4 %all-gather.9.cloned.1.call-done = bf16[16,57,2304]{2,1,0:T(8,128)(2,1)} async-done(((bf16[1,57,2304]{2,1,0:T(8,128)(2,1)}), bf16[16,57,2304]{2,1,0:T(8,128)(2,1)}) %all-gather.9.cloned.1.call-update) | async-done | bytes 4202512 | tf_op jit(solution)/shard_map/all_gather | solution.py:132
  146.9 0.8 slice_convert_fusion
  147.7 0.2 slice.29
  147.9 0.2 slice.30
  148.1 0.1 select_n.198
  148.2 2.2 %slice-done = bf16[16,56,2304]{2,1,0:T(8,128)(2,1)S(1)} async-done(((bf16[16,57,2304]{2,1,0:T(8,128)(2,1)}), bf16[16,56,2304]{2,1,0:T(8,128)(2,1)S(1)}, s32[]{:S(2)}) %slice-start) | async-done | bytes 4128792 | tf_op jit(solution)/shard_map/slice | solution.py:134
  150.4 6.0 %fusion.4 = f32[768,2304]{1,0:T(8,128)} fusion(bf16[896,2304]{1,0:T(8,128)(2,1)S(1)} %bitcast.39, s32[896]{0:T(1024)S(1)} %select_n.198), kind=kOutput, calls=%fused_computation.13 | convolution fusion | flops 3171581952 | bytes 11210240 | tf_op jit(solution)/shard_map/dot_general | solution.py:143
  156.3 8.6 %reshape.527 = f32[256,6912]{1,0:T(8,128)} reshape(f32[768,2304]{1,0:T(8,128)} %fusion.4) | data formatting | bytes 14155776 | tf_op jit(solution)/shard_map/reshape | solution.py:146
  (52 shorter events, 0.9 us)
Async XLA Ops:
  7.2 6.0 %copy-start = (f32[16,384]{1,0:T(8,128)S(1)}, f32[16,384]{1,0:T(8,128)}, u32[]{:S(2)}) copy-start(f32[16,384]{1,0:T(8,128)} %param.15) | copy-start | bytes 73732
  7.2 82.5 %all-gather.7.cloned.1.call-start = ((), (), s32[]{:S(2)}) async-start(), calls=%async_computation | async-start | bytes 1253376 | tf_op jit(solution)/shard_map/all_gather | solution.py:86
  7.7 20.4 %copy-start.1 = (s32[16]{0:T(128)S(1)}, s32[16]{0:T(128)}, u32[]{:S(2)}) copy-start(s32[16]{0:T(128)} %param.17) | copy-start | bytes 196
  7.7 20.7 %copy-start.3 = (s32[16]{0:T(128)S(1)}, s32[16]{0:T(128)}, u32[]{:S(2)}) copy-start(s32[16]{0:T(128)} %param.19) | copy-start | bytes 196
  7.7 20.7 %copy-start.5 = (s32[16,1]{0,1:T(1,128)S(1)}, s32[16,1]{0,1:T(1,128)}, u32[]{:S(2)}) copy-start(s32[16,1]{0,1:T(1,128)} %param.21) | copy-start | bytes 196
  7.8 20.8 %copy-start.4 = (s32[16]{0:T(128)S(1)}, s32[16]{0:T(128)}, u32[]{:S(2)}) copy-start(s32[16]{0:T(128)} %param.23) | copy-start | bytes 196
  12.9 134.0 %all-gather.9.cloned.1.call-start = ((), (), s32[]{:S(2)}) async-start(), calls=%async_computation.1 | async-start | bytes 5013504 | tf_op jit(solution)/shard_map/all_gather | solution.py:132
  31.8 39.7 %copy-start.6 = (s32[32]{0:T(128)S(1)}, s32[32]{0:T(128)}, u32[]{:S(2)}) copy-start(s32[32]{0:T(128)} %param.22) | copy-start | bytes 388
  31.8 39.7 %copy-start.7 = (s32[32,1]{0,1:T(1,128)S(1)}, s32[32,1]{0,1:T(1,128)}, u32[]{:S(2)}) copy-start(s32[32,1]{0,1:T(1,128)} %param.20) | copy-start | bytes 388
  31.8 40.2 %copy-start.2 = (s32[32]{0:T(128)S(1)}, s32[32]{0:T(128)}, u32[]{:S(2)}) copy-start(s32[32]{0:T(128)} %param.16) | copy-start | bytes 388
  36.6 37.8 %copy-start.8 = (s32[32]{0:T(128)S(1)}, s32[32]{0:T(128)}, u32[]{:S(2)}) copy-start(s32[32]{0:T(128)} %param.18) | copy-start | bytes 388
  148.2 2.2 %slice-start = ((bf16[16,57,2304]{2,1,0:T(8,128)(2,1)}), bf16[16,56,2304]{2,1,0:T(8,128)(2,1)S(1)}, s32[]{:S(2)}) async-start(bf16[16,57,2304]{2,1,0:T(8,128)(2,1)} %all-gather.9.cloned.1.call-done), calls=%async_computation.2 | async-start | bytes 8257536 | tf_op jit(solution)/shard_map/slice | solution.py:134
Sparse Core Ops, SparseCore 0:
  13.0 44.4 all-gather.6
  89.8 57.1 all-gather.8

commit v2 on v1

--- a/solution.py
+++ b/solution.py
@@ -2,6 +2,8 @@
 import jax.numpy as jnp
 from jax import lax
 from jax.sharding import PartitionSpec as P
+from jax.experimental import pallas as pl
+from jax.experimental.pallas import tpu as pltpu
 
 CROSS_CAP = 3
 
@@ -45,6 +47,66 @@
 
 def coarse_terms(row_side, products):
     return jnp.einsum("rci,rdi->rcd", row_side, products, preferred_element_type=jnp.float32)
+
+
+def direct_gather(x, axis, other, order, collective_id):
+    n = lax.axis_size(axis)
+
+    def device(peer):
+        here = {axis: peer, other: lax.axis_index(other)}
+        return tuple(here[name] for name in order)
+
+    def kernel(x_ref, o_ref, send_sem, recv_sem, local_sem):
+        me = lax.axis_index(axis)
+        barrier = pltpu.get_barrier_semaphore()
+        for step in range(1, n):
+            pl.semaphore_signal(
+                barrier, 1, device_id=device(lax.rem(me + step, n)),
+                device_id_type=pl.DeviceIdType.MESH,
+            )
+        pl.semaphore_wait(barrier, n - 1)
+        local = pltpu.make_async_copy(x_ref, o_ref.at[me], local_sem)
+        local.start()
+        sends = []
+        for step in range(1, n):
+            copy = pltpu.make_async_remote_copy(
+                src_ref=x_ref,
+                dst_ref=o_ref.at[me],
+                send_sem=send_sem.at[step],
+                recv_sem=recv_sem.at[step],
+                device_id=device(lax.rem(me + step, n)),
+                device_id_type=pl.DeviceIdType.MESH,
+            )
+            copy.start()
+            sends.append(copy)
+        for copy in sends:
+            copy.wait_send()
+        for step in range(1, n):
+            source = lax.rem(me - step + n, n)
+            pltpu.make_async_remote_copy(
+                src_ref=x_ref,
+                dst_ref=o_ref.at[source],
+                send_sem=send_sem.at[step],
+                recv_sem=recv_sem.at[step],
+                device_id=device(source),
+                device_id_type=pl.DeviceIdType.MESH,
+            ).wait_recv()
+        local.wait()
+
+    return pl.pallas_call(
+        kernel,
+        out_shape=jax.ShapeDtypeStruct((n,) + x.shape, x.dtype),
+        in_specs=[pl.BlockSpec(memory_space=pl.ANY)],
+        out_specs=pl.BlockSpec(memory_space=pl.ANY),
+        scratch_shapes=[
+            pltpu.SemaphoreType.DMA((n,)),
+            pltpu.SemaphoreType.DMA((n,)),
+            pltpu.SemaphoreType.DMA,
+        ],
+        compiler_params=pltpu.CompilerParams(
+            collective_id=collective_id, has_side_effects=True
+        ),
+    )(x)
 
 
 def id_row(values, width):
@@ -77,8 +139,9 @@
     inner_count = face_in.shape[0]
     cross_count = face_cross.shape[0]
 
-    metric_dom = lax.all_gather(metric, "dom", axis=0, tiled=True)
-    metric_grp = lax.all_gather(metric, "grp", axis=0, tiled=True)
+    order = ("grp", "dom")
+    metric_dom = direct_gather(metric, "dom", "grp", order, 0).reshape(-1, metric.shape[1])
+    metric_grp = direct_gather(metric, "grp", "dom", order, 1).reshape(-1, metric.shape[1])
 
     diag_side = plain_restrictor(metric)
     diag_c = coarse_terms(diag_side, one_sided(diag_blocks, diag_side))
@@ -95,7 +158,7 @@
     cross_packet = jnp.concatenate(
         (cross_c.astype(jnp.bfloat16), id_row(cross_ids, square)), axis=0
     )
-    cross_got = lax.all_gather(cross_packet, "grp", axis=0)
+    cross_got = direct_gather(cross_packet, "grp", "dom", order, 2)
     got_rows = cross_got[:, :cross_count, :]
     got_ids = cross_got[:, cross_count, : 2 * cross_count].astype(jnp.int32)
     got_peer = got_ids[:, 0::2]
@@ -137,10 +200,14 @@
     lo = codes[:, 1::2].reshape(-1)
     got_slot = jnp.where(hi >= 0, hi * 32 + lo, -1)
     group_slots = group_width * slots_dev
-    onehot = (
-        jnp.arange(group_slots, dtype=jnp.int32)[:, None] == got_slot[None, :]
-    ).astype(jnp.bfloat16)
-    face = jnp.dot(onehot, contrib, preferred_element_type=jnp.float32)
+    group_elems = group_width * elem_count
+    faces = []
+    for slot in range(3):
+        onehot = (
+            (jnp.arange(group_elems, dtype=jnp.int32) * 3 + slot)[:, None] == got_slot[None, :]
+        ).astype(jnp.bfloat16)
+        faces.append(jnp.dot(onehot, contrib, preferred_element_type=jnp.float32))
+    face = jnp.concatenate(faces, axis=1)
 
     coarse_diag = diag_all.astype(jnp.float32)
     coarse_face = face.reshape(group_width * elem_count, 3 * square)

time: 172 us -> 152 us (0.88)
  blocking collectives: 48.4 us -> 0 us
  Pallas kernels: 0 us -> 36.9 us
  local copies, waits for them, and re-layouts: 15.2 us -> 6.87 us
  other arithmetic: 14.3 us -> 19.1 us
  waiting for transfers between devices: 54.5 us -> 50.1 us
    all_gather x3 -> x0, blocking collectives: 48.4 us -> none  [the longest x1 20.3 us: per_device(): metric_dom = lax.all_gather(metric, 'dom', axis=0, tiled=True)]
    pallas_call x0 -> x3, Pallas kernels: none -> 36.9 us  [direct_gather(): pl.pallas_call(kernel, out_shape=jax.ShapeDtypeStruct((n,) + x.shape, x.d...]
    reshape x1 -> x0, local copies, waits for them, and re-layouts: 8.64 us -> none  [per_device(): coarse_face = face.reshape(group_width * elem_count, 3 * square)]
    all_gather x1, waiting for transfers between devices: 54.4 us -> 50 us  [per_device(): face_all = lax.all_gather(face_packet, 'dom', axis=0)]
    concatenate x0 -> x2, other arithmetic: none -> 3.87 us  [the longest x1 3.21 us: per_device(): face = jnp.concatenate(faces, axis=1)]
    dot_general x1 -> x3, matrix products: 5.97 us -> 4.47 us  [per_device(): faces.append(jnp.dot(onehot, contrib, preferred_element_type=jnp.float32))]
  transfers between devices with their start and end apart: 2 -> 2, of which waited for: 1 -> 1; matrix products, arithmetic and copies ran while one was open for 18% -> 22% of each run, Pallas kernels for 0% -> 24%
where the time goes in v2:
time: 152 us
  waiting for transfers between devices  50.1 us (33%)
  Pallas kernels  36.9 us (24%)
  matrix products  24.5 us (16%)
  other arithmetic  19.1 us (13%)
  between operations  14.5 us (10%)
  local copies, waits for them, and re-layouts  6.87 us (5%)
    all_gather x1, waiting for transfers between devices, per_device(): face_all = lax.all_gather(face_packet, 'dom', axis=0)  50 us
    pallas_call x3, Pallas kernels, direct_gather(): pl.pallas_call(kernel, out_shape=jax.ShapeDtypeStruct((n,) + x.shape, x.d...  36.9 us
    dot_general x3, matrix products, coarse_terms(): jnp.einsum('rci,rdi->rcd', row_side, products, preferred_element_type=jnp...  17.5 us
    dot_general x3, matrix products, per_device(): faces.append(jnp.dot(onehot, contrib, preferred_element_type=jnp.float32))  4.47 us
    concatenate x1, other arithmetic, per_device(): face = jnp.concatenate(faces, axis=1)  3.21 us
    mul x2, other arithmetic, restrictor(): full = weights[:, None, :] * table[None]  3.11 us
  transfers between devices with their start and end apart: 2, of which 1 were waited for; matrix products, arithmetic and copies ran while one was open for 22% of the time, Pallas kernels for 24%

profile of v2, /device:TPU:1, one launch (start us, length us, event | category | flops | bytes accessed | tf_op | source)
XLA Modules:
  0.0 152.0 jit_solution(6976109541555202762)
XLA Ops:
  7.4 0.1 mul.207
  7.5 0.1 broadcast_multiply_fusion.3
  7.6 0.1 mul.210
  7.8 4.3 %fusion.24 = bf16[16,48,48]{2,1,0:T(8,128)(2,1)S(1)} fusion(bf16[16,384,384]{2,1,0:T(8,128)(2,1)} %param.12, f32[48,384]{1,0:T(8,128)S(1)} %mul.210, f32[16,384]{1,0:T(8,128)} %x_ref.3), kind=kOutput, calls=%fused_computation.28 | convolution fusion | flops 256315392 | bytes 4890624 | tf_op jit(solution)/shard_map/rci,rdi->rcd/dot_general | solution.py:49
  12.1 0.9 convert_element_type.106
  13.1 0.1 copy.31
  13.2 8.9 %shard_map.132 = f32[8,16,384]{2,1,0:T(8,128)} custom-call(f32[16,384]{1,0:T(8,128)} %x_ref.3), custom_call_target="tpu_custom_call" | custom-call | tf_op jit(solution)/shard_map/pallas_call | solution.py:96
  22.1 0.1 mul.226
  22.4 0.4 fusion.53
  22.9 1.0 broadcast_multiply_fusion.1
  23.9 0.6 reverse_select_fusion.5
  24.5 0.7 reverse_select_fusion.4
  25.2 0.7 fusion.1
  25.9 0.2 fusion.52
  26.1 4.3 %fusion.25 = bf16[16,48,48]{2,1,0:T(8,128)(2,1)S(1)} fusion(bf16[16,384,384]{2,1,0:T(8,128)(2,1)} %param.14, bf16[16,48,384]{1,0,2:T(8,128)(2,1)S(1)} %bitcast.40, f32[16,384]{1,0:T(8,128)S(1)} %fusion.52, f32[48,384]{1,0:T(8,128)S(1)} %mul.210), kind=kOutput, calls=%fused_computation.29 | convolution fusion | flops 255725568 | bytes 5480448 | tf_op jit(solution)/shard_map/rci,rdi->rcd/dot_general | solution.py:49
  30.5 0.2 convert_element_type.119
  30.7 0.1 copy.36
  30.8 0.1 convert_element_type.120
  30.9 0.7 pad_maximum_fusion.1.x_ref
  31.6 14.2 %shard_map.133 = bf16[8,17,2304]{2,1,0:T(8,128)(2,1)} custom-call(bf16[17,2304]{1,0:T(8,128)(2,1)} %pad_maximum_fusion.1.x_ref), custom_call_target="tpu_custom_call" | custom-call | tf_op jit(solution)/shard_map/pallas_call | solution.py:96
  45.7 0.7 slice_convert_fusion.1
  46.7 0.2 reduce_window_sum.11
  46.8 0.2 fusion.72
  47.1 1.3 convolution_convert_fusion
  48.4 13.8 %shard_map.131 = f32[16,16,384]{2,1,0:T(8,128)} custom-call(f32[16,384]{1,0:T(8,128)} %x_ref.3), custom_call_target="tpu_custom_call" | custom-call | tf_op jit(solution)/shard_map/pallas_call | solution.py:96
  62.2 0.2 select_reduce_fusion
  62.6 0.1 copy.37
  62.7 0.1 convert_element_type.125
  62.9 0.1 reshape.540
  63.0 0.4 fusion.49
  63.4 2.1 %broadcast_multiply_fusion = bf16[32,48,6,4,4,4]{1,0,5,4,3,2:T(8,128)(2,1)S(1)} fusion(f32[48,6,4,4,4]{0,4,3,2,1:T(4,128)S(1)} %broadcast_multiply_fusion.2, f32[32,6,4,4,4]{0,4,3,2,1:T(4,128)S(1)} %bitcast.45), kind=kLoop, calls=%fused_computation.12 | loop fusion | flops 1179648 | bytes 1302528 | tf_op jit(solution)/shard_map/mul | solution.py:21
  65.6 0.3 fusion.47
  65.9 1.3 reverse_select_fusion.2
  67.2 1.5 reverse_select_fusion.1
  68.7 1.1 fusion
  69.8 8.9 %fusion.15 = bf16[32,48,48]{2,1,0:T(8,128)(2,1)} fusion(bf16[32,384,384]{2,1,0:T(8,128)(2,1)} %param.13, bf16[32,48,384]{1,0,2:T(8,128)(2,1)S(1)} %bitcast.39, f32[48,384]{1,0:T(8,128)S(1)} %mul.210, f32[32,384]{1,0:T(8,128)S(1)} %fusion.47), kind=kOutput, calls=%fused_computation.21 | convolution fusion | flops 511451136 | bytes 10887168 | tf_op jit(solution)/shard_map/rci,rdi->rcd/dot_general | solution.py:49
  78.7 1.4 convert_element_type.113
  80.1 0.7 maximum_bitcast_fusion
  80.9 2.8 %convert_element_type.107 = f32[256,2304]{1,0:T(8,128)} convert(bf16[256,2304]{1,0:T(8,128)(2,1)} %all-gather.5.cloned.1.call-done) | non-fusion elementwise | flops 589824 | bytes 3538944 | tf_op jit(solution)/shard_map/convert_element_type | solution.py:212
  83.7 50.0 %all-gather.7.cloned.1.call-done = bf16[16,57,2304]{2,1,0:T(8,128)(2,1)} async-done(((bf16[1,57,2304]{2,1,0:T(8,128)(2,1)}), bf16[16,57,2304]{2,1,0:T(8,128)(2,1)}) %all-gather.7.cloned.1.call-update) | async-done | bytes 4202512 | tf_op jit(solution)/shard_map/all_gather | solution.py:195
  133.8 0.8 slice_convert_fusion
  134.5 0.2 slice.29
  134.7 0.2 slice.30
  135.0 2.4 %slice.33 = bf16[16,56,2304]{2,1,0:T(8,128)(2,1)S(1)} slice(bf16[16,57,2304]{2,1,0:T(8,128)(2,1)} %all-gather.7.cloned.1.call-done), slice={[0:16], [0:56], [0:2304]} | slice | bytes 8257536 | tf_op jit(solution)/shard_map/slice | solution.py:197
  137.4 1.5 fusion.32
  138.9 1.5 fusion.30
  140.4 1.5 fusion.28
  141.9 3.2 %pad_maximum_fusion = f32[256,6912]{1,0:T(8,128)} fusion(f32[256,2304]{1,0:T(8,128)S(1)} %fusion.28, f32[256,2304]{1,0:T(8,128)S(1)} %fusion.30, f32[256,2304]{1,0:T(8,128)S(1)} %fusion.32), kind=kLoop, calls=%fused_computation.3 | loop fusion | flops 3538944 | bytes 14155776 | tf_op jit(solution)/shard_map/concatenate | solution.py:210
  (62 shorter events, 1.3 us)
Async XLA Ops:
  7.2 73.7 %all-gather.5.cloned.1.call-start = ((), (), s32[]{:S(2)}) async-start(), calls=%async_computation | async-start | bytes 1253376 | tf_op jit(solution)/shard_map/all_gather | solution.py:149
  7.7 14.7 %copy-start.1 = (f32[16,384]{1,0:T(8,128)S(1)}, f32[16,384]{1,0:T(8,128)}, u32[]{:S(2)}) copy-start(f32[16,384]{1,0:T(8,128)} %x_ref.3) | copy-start | bytes 73732
  7.7 14.7 %copy-start.4 = (s32[16]{0:T(128)S(1)}, s32[16]{0:T(128)}, u32[]{:S(2)}) copy-start(s32[16]{0:T(128)} %param.17) | copy-start | bytes 196
  7.7 15.0 %copy-start.6 = (s32[16]{0:T(128)S(1)}, s32[16]{0:T(128)}, u32[]{:S(2)}) copy-start(s32[16]{0:T(128)} %param.19) | copy-start | bytes 196
  7.7 15.1 %copy-start.8 = (s32[16,1]{0,1:T(1,128)S(1)}, s32[16,1]{0,1:T(1,128)}, u32[]{:S(2)}) copy-start(s32[16,1]{0,1:T(1,128)} %param.21) | copy-start | bytes 196
  7.8 15.1 %copy-start.7 = (s32[16]{0:T(128)S(1)}, s32[16]{0:T(128)}, u32[]{:S(2)}) copy-start(s32[16]{0:T(128)} %param.23) | copy-start | bytes 196
  12.9 120.8 %all-gather.7.cloned.1.call-start = ((), (), s32[]{:S(2)}) async-start(), calls=%async_computation.1 | async-start | bytes 5013504 | tf_op jit(solution)/shard_map/all_gather | solution.py:195
  24.5 1.4 copy-start.3
  26.1 36.4 %copy-start.9 = (s32[32]{0:T(128)S(1)}, s32[32]{0:T(128)}, u32[]{:S(2)}) copy-start(s32[32]{0:T(128)} %param.22) | copy-start | bytes 388
  26.1 36.4 %copy-start.10 = (s32[32,1]{0,1:T(1,128)S(1)}, s32[32,1]{0,1:T(1,128)}, u32[]{:S(2)}) copy-start(s32[32,1]{0,1:T(1,128)} %param.20) | copy-start | bytes 388
  26.1 36.9 %copy-start.2 = (f32[16,384]{1,0:T(8,128)S(1)}, f32[16,384]{1,0:T(8,128)}, u32[]{:S(2)}) copy-start(f32[16,384]{1,0:T(8,128)} %x_ref.3) | copy-start | bytes 73732
  26.1 36.9 %copy-start.5 = (s32[32]{0:T(128)S(1)}, s32[32]{0:T(128)}, u32[]{:S(2)}) copy-start(s32[32]{0:T(128)} %param.16) | copy-start | bytes 388
  31.6 34.0 %copy-start.11 = (s32[32]{0:T(128)S(1)}, s32[32]{0:T(128)}, u32[]{:S(2)}) copy-start(s32[32]{0:T(128)} %param.18) | copy-start | bytes 388
  62.2 3.4 %copy-start = (f32[16,16,384]{2,1,0:T(8,128)S(1)}, f32[16,16,384]{2,1,0:T(8,128)}, u32[]{:S(2)}) copy-start(f32[16,16,384]{2,1,0:T(8,128)} %shard_map.131) | copy-start | bytes 1179652
Sparse Core Ops, SparseCore 0:
  13.1 46.3 all-gather.4
  80.9 52.7 all-gather.6

commit v3 on v1

--- a/solution.py
+++ b/solution.py
@@ -2,6 +2,8 @@
 import jax.numpy as jnp
 from jax import lax
 from jax.sharding import PartitionSpec as P
+from jax.experimental import pallas as pl
+from jax.experimental.pallas import tpu as pltpu
 
 CROSS_CAP = 3
 
@@ -45,6 +47,80 @@
 
 def coarse_terms(row_side, products):
     return jnp.einsum("rci,rdi->rcd", row_side, products, preferred_element_type=jnp.float32)
+
+
+def direct_gather(x, axes, order, collective_id):
+    sizes = [lax.axis_size(axis) for axis in axes]
+
+    def device(axis, peer):
+        return tuple(peer if name == axis else lax.axis_index(name) for name in order)
+
+    def kernel(x_ref, *rest):
+        outs = rest[: len(axes)]
+        send_sem, recv_sem, local_sem = rest[len(axes):]
+        barrier = pltpu.get_barrier_semaphore()
+        for axis, n in zip(axes, sizes):
+            me = lax.axis_index(axis)
+            for step in range(1, n):
+                pl.semaphore_signal(
+                    barrier, 1, device_id=device(axis, lax.rem(me + step, n)),
+                    device_id_type=pl.DeviceIdType.MESH,
+                )
+        pl.semaphore_wait(barrier, sum(n - 1 for n in sizes))
+        locals_ = []
+        sends = []
+        base = 0
+        for a, (axis, n) in enumerate(zip(axes, sizes)):
+            me = lax.axis_index(axis)
+            local = pltpu.make_async_copy(x_ref, outs[a].at[me], local_sem.at[a])
+            local.start()
+            locals_.append(local)
+            for step in range(1, n):
+                copy = pltpu.make_async_remote_copy(
+                    src_ref=x_ref,
+                    dst_ref=outs[a].at[me],
+                    send_sem=send_sem.at[base + step],
+                    recv_sem=recv_sem.at[base + step],
+                    device_id=device(axis, lax.rem(me + step, n)),
+                    device_id_type=pl.DeviceIdType.MESH,
+                )
+                copy.start()
+                sends.append(copy)
+            base += n
+        for copy in sends:
+            copy.wait_send()
+        base = 0
+        for a, (axis, n) in enumerate(zip(axes, sizes)):
+            me = lax.axis_index(axis)
+            for step in range(1, n):
+                source = lax.rem(me - step + n, n)
+                pltpu.make_async_remote_copy(
+                    src_ref=x_ref,
+                    dst_ref=outs[a].at[source],
+                    send_sem=send_sem.at[base + step],
+                    recv_sem=recv_sem.at[base + step],
+                    device_id=device(axis, source),
+                    device_id_type=pl.DeviceIdType.MESH,
+                ).wait_recv()
+            base += n
+        for local in locals_:
+            local.wait()
+
+    total = sum(sizes)
+    return pl.pallas_call(
+        kernel,
+        out_shape=tuple(jax.ShapeDtypeStruct((n,) + x.shape, x.dtype) for n in sizes),
+        in_specs=[pl.BlockSpec(memory_space=pl.ANY)],
+        out_specs=tuple(pl.BlockSpec(memory_space=pl.ANY) for _ in sizes),
+        scratch_shapes=[
+            pltpu.SemaphoreType.DMA((total,)),
+            pltpu.SemaphoreType.DMA((total,)),
+            pltpu.SemaphoreType.DMA((len(axes),)),
+        ],
+        compiler_params=pltpu.CompilerParams(
+            collective_id=collective_id, has_side_effects=True
+        ),
+    )(x)
 
 
 def id_row(values, width):
@@ -77,13 +153,14 @@
     inner_count = face_in.shape[0]
     cross_count = face_cross.shape[0]
 
-    metric_dom = lax.all_gather(metric, "dom", axis=0, tiled=True)
-    metric_grp = lax.all_gather(metric, "grp", axis=0, tiled=True)
+    order = ("grp", "dom")
+    metric_dom, metric_grp = direct_gather(metric, ("dom", "grp"), order, 0)
+    metric_dom = metric_dom.reshape(-1, metric.shape[1])
+    metric_grp = metric_grp.reshape(-1, metric.shape[1])
 
     diag_side = plain_restrictor(metric)
     diag_c = coarse_terms(diag_side, one_sided(diag_blocks, diag_side))
     diag_rows = diag_c.reshape(elem_count, square).astype(jnp.bfloat16)
-    diag_all = lax.all_gather(diag_rows, "dom", axis=0, tiled=True)
 
     cross_y = one_sided(face_cross, restrictor(pick_rows(source_cross, metric), orient_cross))
     peer_x = peer_cross[:, 0]
@@ -95,7 +172,7 @@
     cross_packet = jnp.concatenate(
         (cross_c.astype(jnp.bfloat16), id_row(cross_ids, square)), axis=0
     )
-    cross_got = lax.all_gather(cross_packet, "grp", axis=0)
+    (cross_got,) = direct_gather(cross_packet, ("grp",), order, 1)
     got_rows = cross_got[:, :cross_count, :]
     got_ids = cross_got[:, cross_count, : 2 * cross_count].astype(jnp.int32)
     got_peer = got_ids[:, 0::2]
@@ -127,22 +204,27 @@
         (jnp.where(valid, slots // 32, -1), jnp.where(valid, slots % 32, 0)), axis=1
     )
     face_packet = jnp.concatenate(
-        (inner_c.astype(jnp.bfloat16), mine_rows, id_row(slot_code, square)), axis=0
+        (id_row(slot_code, square), diag_rows, inner_c.astype(jnp.bfloat16), mine_rows), axis=0
     )
     face_all = lax.all_gather(face_packet, "dom", axis=0)
     contrib_count = slots.shape[0]
-    contrib = face_all[:, :contrib_count, :].reshape(group_width * contrib_count, square)
-    codes = face_all[:, contrib_count, : 2 * contrib_count].astype(jnp.int32)
-    hi = codes[:, 0::2].reshape(-1)
-    lo = codes[:, 1::2].reshape(-1)
+    packet_rows = face_packet.shape[0]
+    contrib = face_all.reshape(group_width * packet_rows, square)
+    codes = face_all[:, 0, : 2 * contrib_count].astype(jnp.int32)
+    hi = jnp.pad(codes[:, 0::2], ((0, 0), (1 + elem_count, 0)), constant_values=-1).reshape(-1)
+    lo = jnp.pad(codes[:, 1::2], ((0, 0), (1 + elem_count, 0))).reshape(-1)
     got_slot = jnp.where(hi >= 0, hi * 32 + lo, -1)
     group_slots = group_width * slots_dev
-    onehot = (
-        jnp.arange(group_slots, dtype=jnp.int32)[:, None] == got_slot[None, :]
-    ).astype(jnp.bfloat16)
-    face = jnp.dot(onehot, contrib, preferred_element_type=jnp.float32)
-
-    coarse_diag = diag_all.astype(jnp.float32)
+    group_elems = group_width * elem_count
+    faces = []
+    for slot in range(3):
+        onehot = (
+            (jnp.arange(group_elems, dtype=jnp.int32) * 3 + slot)[:, None] == got_slot[None, :]
+        ).astype(jnp.bfloat16)
+        faces.append(jnp.dot(onehot, contrib, preferred_element_type=jnp.float32))
+    face = jnp.concatenate(faces, axis=1)
+
+    coarse_diag = face_all[:, 1 : 1 + elem_count, :].reshape(-1, square).astype(jnp.float32)
     coarse_face = face.reshape(group_width * elem_count, 3 * square)
     return (coarse_diag, coarse_face)
 

time: 172 us -> 164 us (0.953)
  blocking collectives: 48.4 us -> 0 us
  Pallas kernels: 0 us -> 29.8 us
  other arithmetic: 14.3 us -> 20.1 us
  matrix products: 24.8 us -> 29.8 us
  local copies, waits for them, and re-layouts: 15.2 us -> 10.7 us
  waiting for transfers between devices: 54.5 us -> 58 us
    all_gather x3 -> x0, blocking collectives: 48.4 us -> none  [the longest x1 20.3 us: per_device(): metric_dom = lax.all_gather(metric, 'dom', axis=0, tiled=True)]
    pallas_call x0 -> x2, Pallas kernels: none -> 29.8 us  [direct_gather(): pl.pallas_call(kernel, out_shape=tuple((jax.ShapeDtypeStruct((n,) + x.sha...]
    reshape x1 -> x0, local copies, waits for them, and re-layouts: 8.64 us -> none  [per_device(): coarse_face = face.reshape(group_width * elem_count, 3 * square)]
    unnamed x18 -> x15, local copies, waits for them, and re-layouts: 0.05 us -> 5.11 us
    concatenate x0 -> x3, other arithmetic: none -> 3.89 us  [the longest x1 3.21 us: per_device(): face = jnp.concatenate(faces, axis=1)]
    all_gather x1, waiting for transfers between devices: 54.4 us -> 58 us  [per_device(): face_all = lax.all_gather(face_packet, 'dom', axis=0)]
    dot_general x1 -> x3, matrix products: 5.97 us -> 8.27 us  [per_device(): faces.append(jnp.dot(onehot, contrib, preferred_element_type=jnp.float32))]
  transfers between devices with their start and end apart: 2 -> 1, of which waited for: 1 -> 1; matrix products, arithmetic and copies ran while one was open for 18% -> 0% of each run, Pallas kernels for 0% -> 0%
where the time goes in v3:
time: 164 us; the launch traced here: 163 us
  waiting for transfers between devices  58 us (35%)
  Pallas kernels  29.8 us (18%)
  matrix products  29.8 us (18%)
  other arithmetic  20.1 us (12%)
  between operations  14.4 us (9%)
  local copies, waits for them, and re-layouts  10.7 us (7%)
    all_gather x1, waiting for transfers between devices, per_device(): face_all = lax.all_gather(face_packet, 'dom', axis=0)  58 us
    pallas_call x2, Pallas kernels, direct_gather(): pl.pallas_call(kernel, out_shape=tuple((jax.ShapeDtypeStruct((n,) + x.sha...  29.8 us
    dot_general x3, matrix products, coarse_terms(): jnp.einsum('rci,rdi->rcd', row_side, products, preferred_element_type=jnp...  17.4 us
    dot_general x3, matrix products, per_device(): faces.append(jnp.dot(onehot, contrib, preferred_element_type=jnp.float32))  8.27 us
    unnamed x15, local copies, waits for them, and re-layouts  5.11 us
  transfers between devices with their start and end apart: 1, of which 1 were waited for; matrix products, arithmetic and copies ran while one was open for 0% of the time, Pallas kernels for 0%

profile of v3, /device:TPU:1, one launch (start us, length us, event | category | flops | bytes accessed | tf_op | source)
XLA Modules:
  0.0 163.0 jit_solution(394874942518019685)
XLA Ops:
  7.5 0.1 mul.212
  7.8 0.7 convert.16
  8.5 0.7 bitcast_add_fusion.1
  9.2 0.7 fusion.60
  9.9 0.1 copy.34
  10.0 0.1 convert_element_type.112
  10.4 14.8 %shard_map.131 = (f32[16,16,384]{2,1,0:T(8,128)}, f32[8,16,384]{2,1,0:T(8,128)}) custom-call(f32[16,384]{1,0:T(8,128)} %x_ref.1), custom_call_target="tpu_custom_call" | custom-call | tf_op jit(solution)/shard_map/pallas_call | solution.py:110
  25.1 1.1 fusion.53
  26.3 0.1 mul.224
  26.4 1.1 fusion.52
  27.6 1.0 broadcast_multiply_fusion.1
  28.6 0.6 reverse_select_fusion.5
  29.2 0.7 reverse_select_fusion.4
  29.9 0.7 fusion.1
  30.6 4.3 %fusion.31 = bf16[16,48,48]{2,1,0:T(8,128)(2,1)S(1)} fusion(bf16[16,384,384]{2,1,0:T(8,128)(2,1)} %param.14, bf16[16,48,384]{1,0,2:T(8,128)(2,1)S(1)} %bitcast.42, f32[48,384]{1,0:T(8,128)S(1)} %mul.215, f32[16,384]{1,0:T(8,128)S(1)} %fusion.52), kind=kOutput, calls=%fused_computation.36 | convolution fusion | flops 255725568 | bytes 5480448 | tf_op jit(solution)/shard_map/rci,rdi->rcd/dot_general | solution.py:49
  34.9 0.2 convert_element_type.111
  35.1 0.7 pad_maximum_fusion.1.x_ref
  35.7 15.1 %shard_map.132 = bf16[8,17,2304]{2,1,0:T(8,128)(2,1)} custom-call(bf16[17,2304]{1,0:T(8,128)(2,1)} %pad_maximum_fusion.1.x_ref), custom_call_target="tpu_custom_call" | custom-call | tf_op jit(solution)/shard_map/pallas_call | solution.py:110
  50.8 0.7 slice_convert_fusion.1
  51.7 0.2 reduce_window_sum.11
  51.9 1.3 convolution_convert_fusion
  53.2 0.2 fusion.73
  53.5 4.2 %fusion.30 = bf16[16,48,48]{2,1,0:T(8,128)(2,1)S(1)} fusion(bf16[16,384,384]{2,1,0:T(8,128)(2,1)} %param.12, f32[16,384]{1,0:T(8,128)S(1)} %copy-done.1, f32[48,384]{1,0:T(8,128)S(1)} %mul.215), kind=kOutput, calls=%fused_computation.35 | convolution fusion | flops 256315392 | bytes 4890624 | tf_op jit(solution)/shard_map/rci,rdi->rcd/dot_general | solution.py:49
  57.8 0.2 convert_element_type.120
  58.0 0.4 fusion.50
  58.5 0.2 select_reduce_fusion
  58.9 0.1 copy.35
  59.0 0.1 convert_element_type.116
  59.2 2.1 %broadcast_multiply_fusion = bf16[32,48,6,4,4,4]{1,0,5,4,3,2:T(8,128)(2,1)S(1)} fusion(f32[48,6,4,4,4]{0,4,3,2,1:T(4,128)S(1)} %broadcast_multiply_fusion.2, f32[32,6,4,4,4]{0,4,3,2,1:T(4,128)S(1)} %bitcast.43), kind=kLoop, calls=%fused_computation.12 | loop fusion | flops 1179648 | bytes 1302528 | tf_op jit(solution)/shard_map/mul | solution.py:21
  61.3 0.3 fusion.47
  61.6 1.3 reverse_select_fusion.2
  62.9 1.5 reverse_select_fusion.1
  64.4 1.1 fusion
  65.6 8.9 %fusion.21 = bf16[32,48,48]{2,1,0:T(8,128)(2,1)} fusion(bf16[32,384,384]{2,1,0:T(8,128)(2,1)} %param.13, bf16[32,48,384]{1,0,2:T(8,128)(2,1)S(1)} %bitcast.41, f32[48,384]{1,0:T(8,128)S(1)} %mul.215, f32[32,384]{1,0:T(8,128)S(1)} %fusion.47), kind=kOutput, calls=%fused_computation.27 | convolution fusion | flops 511451136 | bytes 10887168 | tf_op jit(solution)/shard_map/rci,rdi->rcd/dot_general | solution.py:49
  74.4 1.4 convert_element_type.126
  75.8 0.8 maximum_bitcast_fusion
  76.7 58.0 %all-gather.4.cloned.1.call-done = bf16[16,73,2304]{2,1,0:T(8,128)(2,1)} async-done(((bf16[1,73,2304]{2,1,0:T(8,128)(2,1)}), bf16[16,73,2304]{2,1,0:T(8,128)(2,1)}) %all-gather.4.cloned.1.call-update) | async-done | bytes 5382160 | tf_op jit(solution)/shard_map/all_gather | solution.py:209
  134.7 0.8 slice_convert_fusion
  135.5 0.2 slice.31
  135.7 0.2 slice.30
  135.9 0.1 select_n.198
  136.0 1.9 %slice.32 = bf16[16,16,2304]{2,1,0:T(8,128)(2,1)S(1)} slice(bf16[16,73,2304]{2,1,0:T(8,128)(2,1)} %all-gather.4.cloned.1.call-done), slice={[0:16], [1:17], [0:2304]} | slice | bytes 2359296 | tf_op jit(solution)/shard_map/slice | solution.py:227
  137.9 1.6 %bitcast_convert_fusion = f32[256,2304]{1,0:T(8,128)} fusion(bf16[16,16,2304]{2,1,0:T(8,128)(2,1)S(1)} %slice.32), kind=kLoop, calls=%fused_computation.30 | loop fusion | flops 589824 | bytes 3538944 | tf_op jit(solution)/shard_map/convert_element_type | solution.py:227
  139.6 5.1 %reshape.551 = bf16[1168,2304]{1,0:T(8,128)(2,1)} reshape(bf16[16,73,2304]{2,1,0:T(8,128)(2,1)} %all-gather.4.cloned.1.call-done) | data formatting | bytes 10764288
  144.6 4.5 %fusion.16 = f32[256,2304]{1,0:T(8,128)S(1)} fusion(bf16[1168,2304]{1,0:T(8,128)(2,1)} %reshape.551, s32[1168]{0:T(1024)S(1)} %select_n.198, s32[256]{0:T(256)S(1)} %iota_multiply_fusion), kind=kOutput, calls=%fused_computation.24 | convolution fusion | flops 1378127872 | bytes 7747136 | tf_op jit(solution)/shard_map/dot_general | solution.py:224
  149.1 1.9 %fusion.12 = f32[256,2304]{1,0:T(8,128)S(1)} fusion(bf16[1168,2304]{1,0:T(8,128)(2,1)S(1)} %copy-done, s32[1168]{0:T(1024)S(1)} %select_n.198, s32[256]{0:T(256)S(1)} %fusion.57), kind=kOutput, calls=%fused_computation.20 | convolution fusion | flops 1378127872 | bytes 7747136 | tf_op jit(solution)/shard_map/dot_general | solution.py:224
  151.0 1.9 %fusion.14 = f32[256,2304]{1,0:T(8,128)S(1)} fusion(bf16[1168,2304]{1,0:T(8,128)(2,1)S(1)} %copy-done, s32[1168]{0:T(1024)S(1)} %select_n.198, s32[256]{0:T(256)S(1)} %fusion.58), kind=kOutput, calls=%fused_computation.22 | convolution fusion | flops 1378127872 | bytes 7747136 | tf_op jit(solution)/shard_map/dot_general | solution.py:224
  152.9 3.2 %pad_maximum_fusion = f32[256,6912]{1,0:T(8,128)} fusion(f32[256,2304]{1,0:T(8,128)S(1)} %fusion.12, f32[256,2304]{1,0:T(8,128)S(1)} %fusion.14, f32[256,2304]{1,0:T(8,128)S(1)} %fusion.16), kind=kLoop, calls=%fused_computation.3 | loop fusion | flops 3538944 | bytes 14155776 | tf_op jit(solution)/shard_map/concatenate | solution.py:225
  (49 shorter events, 1.5 us)
Async XLA Ops:
  7.2 127.6 %all-gather.4.cloned.1.call-start = ((), (), s32[]{:S(2)}) async-start(), calls=%async_computation | async-start | bytes 6266880 | tf_op jit(solution)/shard_map/all_gather | solution.py:209
  30.6 22.9 %copy-start.4 = (s32[32]{0:T(128)S(1)}, s32[32]{0:T(128)}, u32[]{:S(2)}) copy-start(s32[32]{0:T(128)} %param.18) | copy-start | bytes 388
  30.6 22.9 %copy-start.1 = (f32[16,384]{1,0:T(8,128)S(1)}, f32[16,384]{1,0:T(8,128)}, u32[]{:S(2)}) copy-start(f32[16,384]{1,0:T(8,128)} %x_ref.1) | copy-start | bytes 73732
  53.5 4.5 %copy-start.3 = (s32[32]{0:T(128)S(1)}, s32[32]{0:T(128)}, u32[]{:S(2)}) copy-start(s32[32]{0:T(128)} %param.16) | copy-start | bytes 388
  53.5 5.3 %copy-start.5 = (s32[32]{0:T(128)S(1)}, s32[32]{0:T(128)}, u32[]{:S(2)}) copy-start(s32[32]{0:T(128)} %param.22) | copy-start | bytes 388
  53.5 5.3 %copy-start.6 = (s32[32,1]{0,1:T(1,128)S(1)}, s32[32,1]{0,1:T(1,128)}, u32[]{:S(2)}) copy-start(s32[32,1]{0,1:T(1,128)} %param.20) | copy-start | bytes 388
  57.8 3.6 %copy-start.2 = (f32[16,16,384]{2,1,0:T(8,128)S(1)}, f32[16,16,384]{2,1,0:T(8,128)}, u32[]{:S(2)}) copy-start(f32[16,16,384]{2,1,0:T(8,128)} %get-tuple-element.5) | copy-start | bytes 1179652
  144.6 4.5 %copy-start = (bf16[1168,2304]{1,0:T(8,128)(2,1)S(1)}, bf16[1168,2304]{1,0:T(8,128)(2,1)}, u32[]{:S(2)}) copy-start(bf16[1168,2304]{1,0:T(8,128)(2,1)} %reshape.551) | copy-start | bytes 16146436
Sparse Core Ops, SparseCore 0:
  76.8 57.8 all-gather.3

commit v4 on v3

--- a/solution.py
+++ b/solution.py
@@ -154,77 +154,77 @@
     cross_count = face_cross.shape[0]
 
     order = ("grp", "dom")
-    metric_dom, metric_grp = direct_gather(metric, ("dom", "grp"), order, 0)
-    metric_dom = metric_dom.reshape(-1, metric.shape[1])
-    metric_grp = metric_grp.reshape(-1, metric.shape[1])
-
-    diag_side = plain_restrictor(metric)
-    diag_c = coarse_terms(diag_side, one_sided(diag_blocks, diag_side))
-    diag_rows = diag_c.reshape(elem_count, square).astype(jnp.bfloat16)
-
-    cross_y = one_sided(face_cross, restrictor(pick_rows(source_cross, metric), orient_cross))
     peer_x = peer_cross[:, 0]
-    cross_row_side = plain_restrictor(
-        pick_rows(peer_x * elem_count + target_cross // 3, metric_grp)
-    )
-    cross_c = coarse_terms(cross_row_side, cross_y).reshape(cross_count, square)
-    cross_ids = jnp.stack((peer_x, target_cross), axis=1)
-    cross_packet = jnp.concatenate(
-        (cross_c.astype(jnp.bfloat16), id_row(cross_ids, square)), axis=0
-    )
-    (cross_got,) = direct_gather(cross_packet, ("grp",), order, 1)
-    got_rows = cross_got[:, :cross_count, :]
-    got_ids = cross_got[:, cross_count, : 2 * cross_count].astype(jnp.int32)
-    got_peer = got_ids[:, 0::2]
-    got_target = got_ids[:, 1::2]
+    peer_i = peer_in[:, 0]
+    id_cols = jnp.zeros((elem_count, 128), jnp.float32)
+    id_cols = id_cols.at[:cross_count, 0].set(peer_x.astype(jnp.float32))
+    id_cols = id_cols.at[:cross_count, 1].set(target_cross.astype(jnp.float32))
+    metric_ids = jnp.concatenate((metric, id_cols), axis=1)
+    fine = metric.shape[1]
+    dom_got, grp_got = direct_gather(metric_ids, ("dom", "grp"), order, 0)
+    metric_dom = dom_got[:, :, :fine].reshape(-1, fine)
+    metric_grp = grp_got[:, :, :fine].reshape(-1, fine)
+    got_peer = grp_got[:, :cross_count, fine].astype(jnp.int32)
+    got_target = grp_got[:, :cross_count, fine + 1].astype(jnp.int32)
+
     match = got_peer == my_grp
     rank = jnp.cumsum(match.astype(jnp.int32), axis=1) - 1
     picks = match[:, None, :] & (
         rank[:, None, :] == jnp.arange(CROSS_CAP, dtype=jnp.int32)[None, :, None]
     )
-    mine_rows = jnp.einsum(
-        "skr,srq->skq", picks.astype(jnp.bfloat16), got_rows, preferred_element_type=jnp.float32
-    ).astype(jnp.bfloat16).reshape(group_count * CROSS_CAP, square)
     mine_target = jnp.sum(jnp.where(picks, got_target[:, None, :], 0), axis=2)
     mine_slot = jnp.where(
         jnp.any(picks, axis=2), my_dom * slots_dev + mine_target, -1
     ).reshape(-1)
-
-    inner_y = one_sided(face_in, restrictor(pick_rows(source_in, metric), orient_in))
-    peer_i = peer_in[:, 0]
-    inner_row_side = plain_restrictor(
-        pick_rows(peer_i * elem_count + target_in // 3, metric_dom)
-    )
-    inner_c = coarse_terms(inner_row_side, inner_y).reshape(inner_count, square)
     inner_slot = peer_i * slots_dev + target_in
-
     slots = jnp.concatenate((inner_slot, mine_slot), axis=0)
     valid = slots >= 0
     slot_code = jnp.stack(
         (jnp.where(valid, slots // 32, -1), jnp.where(valid, slots % 32, 0)), axis=1
     )
-    face_packet = jnp.concatenate(
-        (id_row(slot_code, square), diag_rows, inner_c.astype(jnp.bfloat16), mine_rows), axis=0
-    )
+
+    diag_side = plain_restrictor(metric)
+    diag_c = coarse_terms(diag_side, one_sided(diag_blocks, diag_side))
+    diag_rows = diag_c.reshape(elem_count, square).astype(jnp.bfloat16)
+    diag_packet = jnp.concatenate((diag_rows, id_row(slot_code, square)), axis=0)
+    diag_all = lax.all_gather(diag_packet, "dom", axis=0)
+
+    cross_y = one_sided(face_cross, restrictor(pick_rows(source_cross, metric), orient_cross))
+    cross_row_side = plain_restrictor(
+        pick_rows(peer_x * elem_count + target_cross // 3, metric_grp)
+    )
+    cross_c = coarse_terms(cross_row_side, cross_y).reshape(cross_count, square)
+    (got_rows,) = direct_gather(cross_c.astype(jnp.bfloat16), ("grp",), order, 1)
+    mine_rows = jnp.einsum(
+        "skr,srq->skq", picks.astype(jnp.bfloat16), got_rows, preferred_element_type=jnp.float32
+    ).astype(jnp.bfloat16).reshape(group_count * CROSS_CAP, square)
+
+    inner_y = one_sided(face_in, restrictor(pick_rows(source_in, metric), orient_in))
+    inner_row_side = plain_restrictor(
+        pick_rows(peer_i * elem_count + target_in // 3, metric_dom)
+    )
+    inner_c = coarse_terms(inner_row_side, inner_y).reshape(inner_count, square)
+
+    face_packet = jnp.concatenate((inner_c.astype(jnp.bfloat16), mine_rows), axis=0)
     face_all = lax.all_gather(face_packet, "dom", axis=0)
     contrib_count = slots.shape[0]
-    packet_rows = face_packet.shape[0]
-    contrib = face_all.reshape(group_width * packet_rows, square)
-    codes = face_all[:, 0, : 2 * contrib_count].astype(jnp.int32)
-    hi = jnp.pad(codes[:, 0::2], ((0, 0), (1 + elem_count, 0)), constant_values=-1).reshape(-1)
-    lo = jnp.pad(codes[:, 1::2], ((0, 0), (1 + elem_count, 0))).reshape(-1)
+    codes = diag_all[:, elem_count, : 2 * contrib_count].astype(jnp.int32)
+    hi = codes[:, 0::2]
+    lo = codes[:, 1::2]
     got_slot = jnp.where(hi >= 0, hi * 32 + lo, -1)
-    group_slots = group_width * slots_dev
     group_elems = group_width * elem_count
     faces = []
     for slot in range(3):
         onehot = (
-            (jnp.arange(group_elems, dtype=jnp.int32) * 3 + slot)[:, None] == got_slot[None, :]
+            (jnp.arange(group_elems, dtype=jnp.int32) * 3 + slot)[:, None, None]
+            == got_slot[None, :, :]
         ).astype(jnp.bfloat16)
-        faces.append(jnp.dot(onehot, contrib, preferred_element_type=jnp.float32))
+        faces.append(
+            jnp.einsum("sdr,drq->sq", onehot, face_all, preferred_element_type=jnp.float32)
+        )
     face = jnp.concatenate(faces, axis=1)
 
-    coarse_diag = face_all[:, 1 : 1 + elem_count, :].reshape(-1, square).astype(jnp.float32)
+    coarse_diag = diag_all[:, :elem_count, :].reshape(-1, square).astype(jnp.float32)
     coarse_face = face.reshape(group_width * elem_count, 3 * square)
     return (coarse_diag, coarse_face)
 

time: 164 us -> 153 us (0.933)
  local copies, waits for them, and re-layouts: 10.7 us -> 4.34 us
  other arithmetic: 20.1 us -> 25.3 us
  waiting for transfers between devices: 58 us -> 53.7 us
  matrix products: 29.8 us -> 26.8 us
  Pallas kernels: 29.8 us -> 27.9 us
    all_gather x1, waiting for transfers between devices: 58 us -> 51.3 us  [per_device(): face_all = lax.all_gather(face_packet, 'dom', axis=0)]
    unnamed x15 -> x20, local copies, waits for them, and re-layouts: 5.11 us -> 0.05 us
    another operation x3 -> x5, other arithmetic: 0.76 us -> 3.32 us
    all_gather x0 -> x1, waiting for transfers between devices: none -> 2.39 us  [per_device(): diag_all = lax.all_gather(diag_packet, 'dom', axis=0)]
    slice x5 -> x6, local copies, waits for them, and re-layouts: 2.42 us -> 0.46 us  [the longest x1 0.19 us: per_device(): lo = codes[:, 1::2]]
    pallas_call x2, Pallas kernels: 29.8 us -> 27.9 us  [direct_gather(): pl.pallas_call(kernel, out_shape=tuple((jax.ShapeDtypeStruct((n,) + x.sha...]
    dot_general x4, matrix products: 2.89 us -> 1.22 us  [pick_rows(): return jnp.dot(picks, table, precision=lax.Precision.HIGHEST)]
    convert_element_type x3 -> x4, other arithmetic: 3.13 us -> 4.28 us  [the longest x1 1.63 us: per_device(): diag_all[:, :elem_count, :].reshape(-1, square).astype(jnp.float32)]
  transfers between devices with their start and end apart: 1 -> 2, of which waited for: 1 -> 2; matrix products, arithmetic and copies ran while one was open for 0% -> 20% of each run, Pallas kernels for 0% -> 8%
where the time goes in v4:
time: 153 us
  waiting for transfers between devices  53.7 us (35%)
  Pallas kernels  27.9 us (18%)
  matrix products  26.8 us (18%)
  other arithmetic  25.3 us (17%)
  between operations  14.5 us (9%)
  local copies, waits for them, and re-layouts  4.34 us (3%)
    all_gather x1, waiting for transfers between devices, per_device(): face_all = lax.all_gather(face_packet, 'dom', axis=0)  51.3 us
    pallas_call x2, Pallas kernels, direct_gather(): pl.pallas_call(kernel, out_shape=tuple((jax.ShapeDtypeStruct((n,) + x.sha...  27.9 us
    dot_general x3, matrix products, coarse_terms(): jnp.einsum('rci,rdi->rcd', row_side, products, preferred_element_type=jnp...  17.4 us
    dot_general x3, matrix products, per_device(): jnp.einsum('sdr,drq->sq', onehot, face_all, preferred_element_type=jnp.fl...  6.88 us
    another operation x5, other arithmetic  3.32 us
    concatenate x1, other arithmetic, per_device(): face = jnp.concatenate(faces, axis=1)  3.21 us
    mul x2, other arithmetic, restrictor(): full = weights[:, None, :] * table[None]  3.11 us
  transfers between devices with their start and end apart: 2, of which 2 were waited for; matrix products, arithmetic and copies ran while one was open for 20% of the time, Pallas kernels for 8%

profile of v4, /device:TPU:1, one launch (start us, length us, event | category | flops | bytes accessed | tf_op | source)
XLA Modules:
  0.0 152.7 jit_solution(14384074630053277327)
XLA Ops:
  7.2 0.6 compare_reduce_fusion.1
  7.8 0.6 compare_reduce_fusion
  8.5 0.7 convert_element_type.130
  9.2 1.3 fusion.56
  10.6 0.6 broadcast_select_fusion
  11.3 0.1 scatter.9
  11.4 1.4 pad_maximum_fusion.2.x_ref
  12.8 15.3 %shard_map.131 = (f32[16,16,512]{2,1,0:T(8,128)}, f32[8,16,512]{2,1,0:T(8,128)}) custom-call(f32[16,512]{1,0:T(8,128)} %pad_maximum_fusion.2.x_ref), custom_call_target="tpu_custom_call" | custom-call | tf_op jit(solution)/shard_map/pallas_call | solution.py:110
  28.1 1.1 convert_reduce_fusion
  29.2 1.1 fusion.43
  30.3 0.2 reduce_window_sum.11
  30.5 0.2 fusion.71
  30.7 0.2 select_reduce_fusion
  31.0 0.7 bitcast_add_fusion.1
  31.9 0.1 convert_element_type.136
  32.6 4.3 %fusion.24 = bf16[16,48,48]{2,1,0:T(8,128)(2,1)S(1)} fusion(bf16[16,384,384]{2,1,0:T(8,128)(2,1)} %param.16, f32[48,384]{1,0:T(8,128)S(1)} %mul.205, f32[16,384]{1,0:T(8,128)} %param.19), kind=kOutput, calls=%fused_computation.32 | convolution fusion | flops 256315392 | bytes 4890624 | tf_op jit(solution)/shard_map/rci,rdi->rcd/dot_general | solution.py:49
  36.9 0.2 convert_element_type.129
  37.1 0.7 maximum_bitcast_fusion
  38.1 0.1 mul.227
  38.4 0.4 fusion.50
  38.9 1.0 broadcast_multiply_fusion.1
  39.9 0.6 reverse_select_fusion.5
  40.5 0.7 reverse_select_fusion.4
  41.2 0.7 fusion.1
  41.9 0.2 fusion.49
  42.1 4.3 %fusion.25 = bf16[16,48,48]{2,1,0:T(8,128)(2,1)S(1)} fusion(bf16[16,384,384]{2,1,0:T(8,128)(2,1)} %param.18, bf16[16,48,384]{1,0,2:T(8,128)(2,1)S(1)} %bitcast.49, f32[16,384]{1,0:T(8,128)S(1)} %fusion.49, f32[48,384]{1,0:T(8,128)S(1)} %mul.205), kind=kOutput, calls=%fused_computation.33 | convolution fusion | flops 255725568 | bytes 5480448 | tf_op jit(solution)/shard_map/rci,rdi->rcd/dot_general | solution.py:49
  46.4 0.8 convert_element_type.152.x_ref
  47.2 12.6 %shard_map.132 = bf16[8,16,2304]{2,1,0:T(8,128)(2,1)} custom-call(bf16[16,2304]{1,0:T(8,128)(2,1)} %convert_element_type.152.x_ref), custom_call_target="tpu_custom_call" | custom-call | tf_op jit(solution)/shard_map/pallas_call | solution.py:110
  59.8 1.3 convolution_convert_fusion
  61.3 0.4 fusion.47
  61.6 2.1 %broadcast_multiply_fusion = bf16[32,48,6,4,4,4]{1,0,5,4,3,2:T(8,128)(2,1)S(1)} fusion(f32[48,6,4,4,4]{0,4,3,2,1:T(4,128)S(1)} %broadcast_multiply_fusion.2, f32[32,6,4,4,4]{0,4,3,2,1:T(4,128)S(1)} %bitcast.51), kind=kLoop, calls=%fused_computation.15 | loop fusion | flops 1179648 | bytes 1302528 | tf_op jit(solution)/shard_map/mul | solution.py:21
  63.8 0.3 fusion.44
  64.1 1.3 reverse_select_fusion.2
  65.4 1.5 reverse_select_fusion.1
  66.9 1.1 fusion
  68.1 8.9 %fusion.15 = bf16[32,48,48]{2,1,0:T(8,128)(2,1)} fusion(bf16[32,384,384]{2,1,0:T(8,128)(2,1)} %param.17, bf16[32,48,384]{1,0,2:T(8,128)(2,1)S(1)} %bitcast.48, f32[48,384]{1,0:T(8,128)S(1)} %mul.205, f32[32,384]{1,0:T(8,128)S(1)} %fusion.44), kind=kOutput, calls=%fused_computation.24 | convolution fusion | flops 511451136 | bytes 10887168 | tf_op jit(solution)/shard_map/rci,rdi->rcd/dot_general | solution.py:49
  77.0 1.4 convert_element_type.146
  78.3 0.7 pad_maximum_fusion.1
  79.1 2.4 %all-gather.8.cloned.1.call-done = bf16[16,17,2304]{2,1,0:T(8,128)(2,1)} async-done(((bf16[1,17,2304]{2,1,0:T(8,128)(2,1)}), bf16[16,17,2304]{2,1,0:T(8,128)(2,1)}) %all-gather.8.cloned.1.call-update) | async-done | bytes 1253392 | tf_op jit(solution)/shard_map/all_gather | solution.py:190
  81.5 0.9 slice_convert_fusion
  82.4 0.2 slice.57
  82.6 0.2 slice.58
  82.8 1.6 %bitcast_convert_fusion = f32[256,2304]{1,0:T(8,128)} fusion(bf16[16,16,2304]{2,1,0:T(8,128)(2,1)S(1)} %slice-done), kind=kLoop, calls=%fused_computation.27 | loop fusion | flops 589824 | bytes 3538944 | tf_op jit(solution)/shard_map/convert_element_type | solution.py:227
  84.4 51.3 %all-gather.6.cloned.1.call-done = bf16[896,2304]{1,0:T(8,128)(2,1)} async-done(((bf16[56,2304]{1,0:T(8,128)(2,1)}), bf16[896,2304]{1,0:T(8,128)(2,1)}) %all-gather.6.cloned.1.call-update) | async-done | bytes 4128784 | tf_op jit(solution)/shard_map/all_gather | solution.py:209
  135.7 3.8 %convolution_bitcast_fusion.2 = f32[256,2304]{1,0:T(8,128)S(1)} fusion(bf16[16,56,2304]{2,1,0:T(8,128)(2,1)} %bitcast.56, s32[16,56]{1,0:T(8,128)S(1)} %add_select_fusion, s32[256]{0:T(256)S(1)} %iota_multiply_fusion), kind=kOutput, calls=%fused_computation.10 | convolution fusion | flops 1057193984 | bytes 6492672 | tf_op jit(solution)/shard_map/sdr,drq->sq/dot_general | solution.py:223
  139.6 1.5 convolution_bitcast_fusion.1
  141.1 1.5 convolution_bitcast_fusion
  142.7 3.2 %pad_maximum_fusion = f32[256,6912]{1,0:T(8,128)} fusion(f32[256,2304]{1,0:T(8,128)S(1)} %convolution_bitcast_fusion, f32[256,2304]{1,0:T(8,128)S(1)} %convolution_bitcast_fusion.1, f32[256,2304]{1,0:T(8,128)S(1)} %convolution_bitcast_fusion.2), kind=kLoop, calls=%fused_computation.3 | loop fusion | flops 3538944 | bytes 14155776 | tf_op jit(solution)/shard_map/concatenate | solution.py:225
  (62 shorter events, 1.8 us)
Async XLA Ops:
  7.2 74.3 %all-gather.8.cloned.1.call-start = ((), (), s32[]{:S(2)}) async-start(), calls=%async_computation.1 | async-start | bytes 1880064 | tf_op jit(solution)/shard_map/all_gather | solution.py:190
  32.3 5.8 %copy-start.1 = (f32[8,16,512]{2,1,0:T(8,128)S(1)}, f32[8,16,512]{2,1,0:T(8,128)}, u32[]{:S(2)}) copy-start(f32[8,16,512]{2,1,0:T(8,128)} %get-tuple-element.28) | copy-start | bytes 786436
  32.5 5.6 %copy-start.8 = (s32[16,1]{0,1:T(1,128)S(1)}, s32[16,1]{0,1:T(1,128)}, u32[]{:S(2)}) copy-start(s32[16,1]{0,1:T(1,128)} %param.25) | copy-start | bytes 196
  32.5 5.6 %copy-start.9 = (s32[16]{0:T(128)S(1)}, s32[16]{0:T(128)}, u32[]{:S(2)}) copy-start(s32[16]{0:T(128)} %param.27) | copy-start | bytes 196
  32.6 5.8 %copy-start = (f32[16,384]{1,0:T(8,128)S(1)}, f32[16,384]{1,0:T(8,128)}, u32[]{:S(2)}) copy-start(f32[16,384]{1,0:T(8,128)} %param.19) | copy-start | bytes 73732
  32.6 5.8 %copy-start.3 = (s32[16]{0:T(128)S(1)}, s32[16]{0:T(128)}, u32[]{:S(2)}) copy-start(s32[16]{0:T(128)} %param.21) | copy-start | bytes 196
  32.6 6.2 %copy-start.5 = (s32[16]{0:T(128)S(1)}, s32[16]{0:T(128)}, u32[]{:S(2)}) copy-start(s32[16]{0:T(128)} %param.23) | copy-start | bytes 196
  37.8 97.9 %all-gather.6.cloned.1.call-start = ((), (), s32[]{:S(2)}) async-start(), calls=%async_computation | async-start | bytes 4386816 | tf_op jit(solution)/shard_map/all_gather | solution.py:209
  42.1 19.2 %copy-start.4 = (s32[32]{0:T(128)S(1)}, s32[32]{0:T(128)}, u32[]{:S(2)}) copy-start(s32[32]{0:T(128)} %param.20) | copy-start | bytes 388
  46.4 17.4 %copy-start.2 = (f32[16,16,512]{2,1,0:T(8,128)S(1)}, f32[16,16,512]{2,1,0:T(8,128)}, u32[]{:S(2)}) copy-start(f32[16,16,512]{2,1,0:T(8,128)} %get-tuple-element.29) | copy-start | bytes 1572868
  59.8 4.3 %copy-start.6 = (s32[32]{0:T(128)S(1)}, s32[32]{0:T(128)}, u32[]{:S(2)}) copy-start(s32[32]{0:T(128)} %param.22) | copy-start | bytes 388
  81.5 1.3 slice-start
  135.7 3.9 %copy-start.7 = (bf16[896,2304]{1,0:T(8,128)(2,1)S(1)}, bf16[896,2304]{1,0:T(8,128)(2,1)}, u32[]{:S(2)}) copy-start(bf16[896,2304]{1,0:T(8,128)(2,1)} %all-gather.6.cloned.1.call-done) | copy-start | bytes 12386308
Sparse Core Ops, SparseCore 0:
  38.0 43.5 all-gather.7
  84.2 51.4 all-gather.5

commit v5 on v4

--- a/solution.py
+++ b/solution.py
@@ -186,8 +186,7 @@
     diag_side = plain_restrictor(metric)
     diag_c = coarse_terms(diag_side, one_sided(diag_blocks, diag_side))
     diag_rows = diag_c.reshape(elem_count, square).astype(jnp.bfloat16)
-    diag_packet = jnp.concatenate((diag_rows, id_row(slot_code, square)), axis=0)
-    diag_all = lax.all_gather(diag_packet, "dom", axis=0)
+    diag_all = lax.all_gather(diag_rows, "dom", axis=0)
 
     cross_y = one_sided(face_cross, restrictor(pick_rows(source_cross, metric), orient_cross))
     cross_row_side = plain_restrictor(
@@ -205,23 +204,29 @@
     )
     inner_c = coarse_terms(inner_row_side, inner_y).reshape(inner_count, square)
 
-    face_packet = jnp.concatenate((inner_c.astype(jnp.bfloat16), mine_rows), axis=0)
+    face_packet = jnp.concatenate(
+        (inner_c.astype(jnp.bfloat16), id_row(slot_code, square)), axis=0
+    )
     face_all = lax.all_gather(face_packet, "dom", axis=0)
+    (cross_all,) = direct_gather(mine_rows, ("dom",), order, 2)
     contrib_count = slots.shape[0]
-    codes = diag_all[:, elem_count, : 2 * contrib_count].astype(jnp.int32)
-    hi = codes[:, 0::2]
-    lo = codes[:, 1::2]
-    got_slot = jnp.where(hi >= 0, hi * 32 + lo, -1)
+    codes = face_all[:, inner_count, : 2 * contrib_count].astype(jnp.int32)
+    got_slot = jnp.where(codes[:, 0::2] >= 0, codes[:, 0::2] * 32 + codes[:, 1::2], -1)
+    inner_got = jnp.pad(got_slot[:, :inner_count], ((0, 0), (0, 1)), constant_values=-1)
+    cross_got = got_slot[:, inner_count:]
     group_elems = group_width * elem_count
     faces = []
     for slot in range(3):
-        onehot = (
-            (jnp.arange(group_elems, dtype=jnp.int32) * 3 + slot)[:, None, None]
-            == got_slot[None, :, :]
-        ).astype(jnp.bfloat16)
-        faces.append(
-            jnp.einsum("sdr,drq->sq", onehot, face_all, preferred_element_type=jnp.float32)
+        wanted = (jnp.arange(group_elems, dtype=jnp.int32) * 3 + slot)[:, None, None]
+        from_inner = jnp.einsum(
+            "sdr,drq->sq", (wanted == inner_got[None]).astype(jnp.bfloat16), face_all,
+            preferred_element_type=jnp.float32,
         )
+        from_cross = jnp.einsum(
+            "sdr,drq->sq", (wanted == cross_got[None]).astype(jnp.bfloat16), cross_all,
+            preferred_element_type=jnp.float32,
+        )
+        faces.append(from_inner + from_cross)
     face = jnp.concatenate(faces, axis=1)
 
     coarse_diag = diag_all[:, :elem_count, :].reshape(-1, square).astype(jnp.float32)

time: 153 us -> 141 us (0.922)
  waiting for transfers between devices: 53.7 us -> 5.49 us
  Pallas kernels: 27.9 us -> 62.8 us
  local copies, waits for them, and re-layouts: 4.34 us -> 8.52 us
  other arithmetic: 25.3 us -> 23.2 us
    all_gather x1, waiting for transfers between devices: 51.3 us -> 5.44 us  [per_device(): face_all = lax.all_gather(face_packet, 'dom', axis=0)]
    pallas_call x2 -> x3, Pallas kernels: 27.9 us -> 62.8 us  [direct_gather(): pl.pallas_call(kernel, out_shape=tuple((jax.ShapeDtypeStruct((n,) + x.sha...]
    all_gather x1, waiting for transfers between devices: 2.39 us -> 0.02 us  [per_device(): diag_all = lax.all_gather(diag_rows, 'dom', axis=0)]
    dot_general x3 -> x6, matrix products: 6.88 us -> 6.39 us  [the longest x3 3.7 us: per_device(): jnp.einsum('sdr,drq->sq', (wanted == inner_got[None]).astype(jnp.bfloat16...]
  transfers between devices with their start and end apart: 2 -> 2, of which waited for: 2 -> 1; matrix products, arithmetic and copies ran while one was open for 20% -> 29% of each run, Pallas kernels for 8% -> 45%
where the time goes in v5:
time: 141 us
  Pallas kernels  62.8 us (45%)
  matrix products  26.3 us (19%)
  other arithmetic  23.2 us (16%)
  between operations  14.5 us (10%)
  local copies, waits for them, and re-layouts  8.52 us (6%)
  waiting for transfers between devices  5.49 us (4%)
    pallas_call x3, Pallas kernels, direct_gather(): pl.pallas_call(kernel, out_shape=tuple((jax.ShapeDtypeStruct((n,) + x.sha...  62.8 us
    dot_general x3, matrix products, coarse_terms(): jnp.einsum('rci,rdi->rcd', row_side, products, preferred_element_type=jnp...  17.4 us
    all_gather x1, waiting for transfers between devices, per_device(): face_all = lax.all_gather(face_packet, 'dom', axis=0)  5.44 us
    dot_general x3, matrix products, per_device(): jnp.einsum('sdr,drq->sq', (wanted == inner_got[None]).astype(jnp.bfloat16...  3.7 us
    concatenate x1, other arithmetic, per_device(): face = jnp.concatenate(faces, axis=1)  3.21 us
    mul x2, other arithmetic, restrictor(): full = weights[:, None, :] * table[None]  3.1 us
    convert_element_type x1, other arithmetic, per_device(): diag_all[:, :elem_count, :].reshape(-1, square).astype(jnp.float32)  2.95 us
  transfers between devices with their start and end apart: 2, of which 1 were waited for; matrix products, arithmetic and copies ran while one was open for 29% of the time, Pallas kernels for 45%

profile of v5, /device:TPU:1, one launch (start us, length us, event | category | flops | bytes accessed | tf_op | source)
XLA Modules:
  0.0 140.8 jit_solution(13216376220905687897)
XLA Ops:
  7.8 4.3 %fusion.27 = bf16[16,48,48]{2,1,0:T(8,128)(2,1)S(1)} fusion(bf16[16,384,384]{2,1,0:T(8,128)(2,1)} %param.16, f32[48,384]{1,0:T(8,128)S(1)} %mul.211, f32[16,384]{1,0:T(8,128)} %param.19), kind=kOutput, calls=%fused_computation.38 | convolution fusion | flops 256315392 | bytes 4890624 | tf_op jit(solution)/shard_map/rci,rdi->rcd/dot_general | solution.py:49
  12.1 0.8 convert_element_type.139
  13.0 0.6 compare_reduce_fusion.1
  13.6 0.6 compare_reduce_fusion
  14.6 0.6 fusion.68
  15.3 0.6 broadcast_select_fusion
  16.1 0.6 pad_maximum_fusion.1.x_ref
  16.7 15.3 %shard_map.131 = (f32[16,16,512]{2,1,0:T(8,128)}, f32[8,16,512]{2,1,0:T(8,128)}) custom-call(f32[16,512]{1,0:T(8,128)} %pad_maximum_fusion.1.x_ref), custom_call_target="tpu_custom_call" | custom-call | tf_op jit(solution)/shard_map/pallas_call | solution.py:110
  32.0 1.1 convert_reduce_fusion
  33.2 1.1 fusion.55
  34.4 0.2 fusion.83
  34.6 0.2 select_reduce_fusion
  35.7 0.4 fusion.58
  36.1 1.0 slice.58
  37.1 1.9 %broadcast_multiply_fusion = bf16[32,48,6,4,4,4]{1,0,5,4,3,2:T(8,128)(2,1)S(1)} fusion(f32[48,6,4,4,4]{0,4,3,2,1:T(4,128)S(1)} %broadcast_multiply_fusion.2, f32[32,6,4,4,4]{0,4,3,2,1:T(4,128)S(1)} %bitcast.65), kind=kLoop, calls=%fused_computation.21 | loop fusion | flops 1179648 | bytes 1302528 | tf_op jit(solution)/shard_map/mul | solution.py:21
  39.1 0.3 fusion.56
  39.4 1.3 reverse_select_fusion.2
  40.7 1.5 %reverse_select_fusion.1 = bf16[32,48,6,4,4,4]{1,0,5,4,3,2:T(8,128)(2,1)S(1)} fusion(bf16[32,48,6,4,4,4]{1,0,5,4,3,2:T(8,128)(2,1)S(1)} %reverse_select_fusion.2, pred[32]{0:T(512)(128)(4,1)S(1)} %get-tuple-element.35), kind=kLoop, calls=%fused_computation.1 | loop fusion | flops 589824 | bytes 2359328 | tf_op jit(solution)/shard_map/jit(_where)/select_n | solution.py:25
  42.2 1.1 fusion
  43.4 8.9 %fusion.18 = bf16[32,48,48]{2,1,0:T(8,128)(2,1)} fusion(bf16[32,384,384]{2,1,0:T(8,128)(2,1)} %param.17, bf16[32,48,384]{1,0,2:T(8,128)(2,1)S(1)} %bitcast.62, f32[48,384]{1,0:T(8,128)S(1)} %mul.211, f32[32,384]{1,0:T(8,128)S(1)} %fusion.56), kind=kOutput, calls=%fused_computation.30 | convolution fusion | flops 511451136 | bytes 10887168 | tf_op jit(solution)/shard_map/rci,rdi->rcd/dot_general | solution.py:49
  52.2 1.4 convert_element_type.149
  53.6 0.7 maximum_bitcast_fusion
  54.3 1.0 slice.66
  55.3 0.4 fusion.62
  55.7 0.2 fusion.61
  55.9 1.2 broadcast_multiply_fusion.1
  57.1 0.6 reverse_select_fusion.5
  57.7 0.7 reverse_select_fusion.4
  58.4 0.7 fusion.4
  59.1 4.3 %fusion.28 = bf16[16,48,48]{2,1,0:T(8,128)(2,1)S(1)} fusion(bf16[16,384,384]{2,1,0:T(8,128)(2,1)} %param.18, bf16[16,48,384]{1,0,2:T(8,128)(2,1)S(1)} %bitcast.63, f32[16,384]{1,0:T(8,128)S(1)} %fusion.61, f32[48,384]{1,0:T(8,128)S(1)} %mul.211), kind=kOutput, calls=%fused_computation.39 | convolution fusion | flops 255725568 | bytes 5480448 | tf_op jit(solution)/shard_map/rci,rdi->rcd/dot_general | solution.py:49
  63.3 0.8 convert_element_type.162.x_ref
  64.2 13.1 %shard_map.132 = bf16[8,16,2304]{2,1,0:T(8,128)(2,1)} custom-call(bf16[16,2304]{1,0:T(8,128)(2,1)} %convert_element_type.162.x_ref), custom_call_target="tpu_custom_call" | custom-call | tf_op jit(solution)/shard_map/pallas_call | solution.py:110
  77.3 1.3 convolution_convert_fusion
  78.6 0.7 reshape.595.x_ref
  79.3 34.4 %shard_map.133 = bf16[16,24,2304]{2,1,0:T(8,128)(2,1)} custom-call(bf16[24,2304]{1,0:T(8,128)(2,1)} %reshape.595.x_ref), custom_call_target="tpu_custom_call" | custom-call | tf_op jit(solution)/shard_map/pallas_call | solution.py:110
  113.8 3.0 %bitcast_convert_fusion = f32[256,2304]{1,0:T(8,128)} fusion(bf16[16,16,2304]{2,1,0:T(8,128)(2,1)} %all-gather.5.cloned.1.call-done), kind=kLoop, calls=%fused_computation.33 | loop fusion | flops 589824 | bytes 3538944 | tf_op jit(solution)/shard_map/convert_element_type | solution.py:232
  116.7 5.4 %all-gather.7.cloned.1.call-done = bf16[16,33,2304]{2,1,0:T(8,128)(2,1)} async-done(((bf16[1,33,2304]{2,1,0:T(8,128)(2,1)}), bf16[16,33,2304]{2,1,0:T(8,128)(2,1)}) %all-gather.7.cloned.1.call-update) | async-done | bytes 2433040 | tf_op jit(solution)/shard_map/all_gather | solution.py:210
  122.2 0.8 slice_convert_fusion
  122.9 0.2 slice.62
  123.1 0.2 slice.63
  123.4 0.9 convolution_bitcast_fusion.2
  124.3 0.9 convolution_bitcast_fusion.1
  125.2 0.9 convolution_bitcast_fusion
  126.1 0.9 copy-done.1
  127.1 1.2 fusion.1
  128.3 1.2 fusion.2
  129.5 1.2 fusion.3
  130.8 3.2 %pad_maximum_fusion = f32[256,6912]{1,0:T(8,128)} fusion(f32[256,2304]{1,0:T(8,128)S(1)} %fusion.3, f32[256,2304]{1,0:T(8,128)S(1)} %fusion.2, f32[256,2304]{1,0:T(8,128)S(1)} %fusion.1), kind=kLoop, calls=%fused_computation.3 | loop fusion | flops 3538944 | bytes 14155776 | tf_op jit(solution)/shard_map/concatenate | solution.py:230
  (69 shorter events, 2.3 us)
Async XLA Ops:
  7.2 106.6 %all-gather.5.cloned.1.call-start = ((), (), s32[]{:S(2)}) async-start(), calls=%async_computation | async-start | bytes 1253376 | tf_op jit(solution)/shard_map/all_gather | solution.py:189
  7.7 6.8 %copy-start.10 = (s32[16,1]{0,1:T(1,128)S(1)}, s32[16,1]{0,1:T(1,128)}, u32[]{:S(2)}) copy-start(s32[16,1]{0,1:T(1,128)} %param.25) | copy-start | bytes 196
  7.7 6.8 %copy-start.11 = (s32[16]{0:T(128)S(1)}, s32[16]{0:T(128)}, u32[]{:S(2)}) copy-start(s32[16]{0:T(128)} %param.27) | copy-start | bytes 196
  7.7 8.4 %copy-start.2 = (f32[16,384]{1,0:T(8,128)S(1)}, f32[16,384]{1,0:T(8,128)}, u32[]{:S(2)}) copy-start(f32[16,384]{1,0:T(8,128)} %param.19) | copy-start | bytes 73732
  7.7 27.2 %copy-start.6 = (s32[32]{0:T(128)S(1)}, s32[32]{0:T(128)}, u32[]{:S(2)}) copy-start(s32[32]{0:T(128)} %param.26) | copy-start | bytes 388
  7.8 27.2 %copy-start.7 = (s32[32,1]{0,1:T(1,128)S(1)}, s32[32,1]{0,1:T(1,128)}, u32[]{:S(2)}) copy-start(s32[32,1]{0,1:T(1,128)} %param.24) | copy-start | bytes 388
  7.8 27.9 %copy-start.3 = (s32[32]{0:T(128)S(1)}, s32[32]{0:T(128)}, u32[]{:S(2)}) copy-start(s32[32]{0:T(128)} %param.20) | copy-start | bytes 388
  7.8 28.3 %copy-start.8 = (s32[32]{0:T(128)S(1)}, s32[32]{0:T(128)}, u32[]{:S(2)}) copy-start(s32[32]{0:T(128)} %param.22) | copy-start | bytes 388
  13.0 109.2 %all-gather.7.cloned.1.call-start = ((), (), s32[]{:S(2)}) async-start(), calls=%async_computation.1 | async-start | bytes 3133440 | tf_op jit(solution)/shard_map/all_gather | solution.py:210
  43.3 12.0 %copy-start.9 = (s32[16]{0:T(128)S(1)}, s32[16]{0:T(128)}, u32[]{:S(2)}) copy-start(s32[16]{0:T(128)} %param.23) | copy-start | bytes 196
  43.4 12.0 %copy-start.4 = (s32[16]{0:T(128)S(1)}, s32[16]{0:T(128)}, u32[]{:S(2)}) copy-start(s32[16]{0:T(128)} %param.21) | copy-start | bytes 196
  79.3 44.1 %copy-start.5 = (pred[33]{0:T(512)(128)(4,1)S(1)}, pred[33]{0:T(512)(128)(4,1)}, u32[]{:S(2)}) copy-start(pred[33]{0:T(512)(128)(4,1)} %constant.205.clone.1) | copy-start | bytes 103
  113.7 9.7 %copy-start = (bf16[16,24,2304]{2,1,0:T(8,128)(2,1)S(1)}, bf16[16,24,2304]{2,1,0:T(8,128)(2,1)}, u32[]{:S(2)}) copy-start(bf16[16,24,2304]{2,1,0:T(8,128)(2,1)} %shard_map.133) | copy-start | bytes 5308420
  125.2 1.8 %copy-start.1 = (bf16[16,33,2304]{2,1,0:T(8,128)(2,1)S(1)}, bf16[16,33,2304]{2,1,0:T(8,128)(2,1)}, u32[]{:S(2)}) copy-start(bf16[16,33,2304]{2,1,0:T(8,128)(2,1)} %all-gather.7.cloned.1.call-done) | copy-start | bytes 7299076
Sparse Core Ops, SparseCore 0:
  13.1 45.0 all-gather.4
  60.9 61.2 all-gather.6

commit v6 on v5

--- a/solution.py
+++ b/solution.py
@@ -123,6 +123,16 @@
     )(x)
 
 
+def slot_codes(slots):
+    valid = slots >= 0
+    return jnp.stack((jnp.where(valid, slots // 32, -1), jnp.where(valid, slots % 32, 0)), axis=1)
+
+
+def read_codes(row, count):
+    codes = row[:, : 2 * count].astype(jnp.int32)
+    return jnp.where(codes[:, 0::2] >= 0, codes[:, 0::2] * 32 + codes[:, 1::2], -1)
+
+
 def id_row(values, width):
     flat = values.reshape(-1).astype(jnp.bfloat16)
     return jnp.pad(flat, (0, width - flat.shape[0]))[None, :]
@@ -156,17 +166,23 @@
     order = ("grp", "dom")
     peer_x = peer_cross[:, 0]
     peer_i = peer_in[:, 0]
+    fine = metric.shape[1]
+    (dom_got,) = direct_gather(metric, ("dom",), order, 0)
+    metric_dom = dom_got.reshape(-1, fine)
+    inner_slot = peer_i * slots_dev + target_in
+
+    diag_side = plain_restrictor(metric)
+    diag_c = coarse_terms(diag_side, one_sided(diag_blocks, diag_side))
+    diag_rows = diag_c.reshape(elem_count, square).astype(jnp.bfloat16)
+    diag_all = lax.all_gather(diag_rows, "dom", axis=0)
+
     id_cols = jnp.zeros((elem_count, 128), jnp.float32)
     id_cols = id_cols.at[:cross_count, 0].set(peer_x.astype(jnp.float32))
     id_cols = id_cols.at[:cross_count, 1].set(target_cross.astype(jnp.float32))
-    metric_ids = jnp.concatenate((metric, id_cols), axis=1)
-    fine = metric.shape[1]
-    dom_got, grp_got = direct_gather(metric_ids, ("dom", "grp"), order, 0)
-    metric_dom = dom_got[:, :, :fine].reshape(-1, fine)
+    (grp_got,) = direct_gather(jnp.concatenate((metric, id_cols), axis=1), ("grp",), order, 3)
     metric_grp = grp_got[:, :, :fine].reshape(-1, fine)
     got_peer = grp_got[:, :cross_count, fine].astype(jnp.int32)
     got_target = grp_got[:, :cross_count, fine + 1].astype(jnp.int32)
-
     match = got_peer == my_grp
     rank = jnp.cumsum(match.astype(jnp.int32), axis=1) - 1
     picks = match[:, None, :] & (
@@ -176,18 +192,6 @@
     mine_slot = jnp.where(
         jnp.any(picks, axis=2), my_dom * slots_dev + mine_target, -1
     ).reshape(-1)
-    inner_slot = peer_i * slots_dev + target_in
-    slots = jnp.concatenate((inner_slot, mine_slot), axis=0)
-    valid = slots >= 0
-    slot_code = jnp.stack(
-        (jnp.where(valid, slots // 32, -1), jnp.where(valid, slots % 32, 0)), axis=1
-    )
-
-    diag_side = plain_restrictor(metric)
-    diag_c = coarse_terms(diag_side, one_sided(diag_blocks, diag_side))
-    diag_rows = diag_c.reshape(elem_count, square).astype(jnp.bfloat16)
-    diag_all = lax.all_gather(diag_rows, "dom", axis=0)
-
     cross_y = one_sided(face_cross, restrictor(pick_rows(source_cross, metric), orient_cross))
     cross_row_side = plain_restrictor(
         pick_rows(peer_x * elem_count + target_cross // 3, metric_grp)
@@ -205,15 +209,18 @@
     inner_c = coarse_terms(inner_row_side, inner_y).reshape(inner_count, square)
 
     face_packet = jnp.concatenate(
-        (inner_c.astype(jnp.bfloat16), id_row(slot_code, square)), axis=0
+        (inner_c.astype(jnp.bfloat16), id_row(slot_codes(inner_slot), square)), axis=0
     )
     face_all = lax.all_gather(face_packet, "dom", axis=0)
-    (cross_all,) = direct_gather(mine_rows, ("dom",), order, 2)
-    contrib_count = slots.shape[0]
-    codes = face_all[:, inner_count, : 2 * contrib_count].astype(jnp.int32)
-    got_slot = jnp.where(codes[:, 0::2] >= 0, codes[:, 0::2] * 32 + codes[:, 1::2], -1)
-    inner_got = jnp.pad(got_slot[:, :inner_count], ((0, 0), (0, 1)), constant_values=-1)
-    cross_got = got_slot[:, inner_count:]
+    cross_packet = jnp.concatenate((mine_rows, id_row(slot_codes(mine_slot), square)), axis=0)
+    (cross_all,) = direct_gather(cross_packet, ("dom",), order, 2)
+    inner_got = jnp.pad(
+        read_codes(face_all[:, inner_count], inner_count), ((0, 0), (0, 1)), constant_values=-1
+    )
+    cross_got = jnp.pad(
+        read_codes(cross_all[:, mine_rows.shape[0]], mine_rows.shape[0]),
+        ((0, 0), (0, 1)), constant_values=-1,
+    )
     group_elems = group_width * elem_count
     faces = []
     for slot in range(3):

time: 141 us -> 163 us (1.16); the launches traced: 141 us -> 160 us
  Pallas kernels: 62.8 us -> 80.2 us
  matrix products: 26.3 us -> 34.8 us
  waiting for transfers between devices: 5.49 us -> 0.06 us
    pallas_call x3 -> x4, Pallas kernels: 62.8 us -> 80.2 us  [direct_gather(): pl.pallas_call(kernel, out_shape=tuple((jax.ShapeDtypeStruct((n,) + x.sha...]
    all_gather x1, waiting for transfers between devices: 5.44 us -> 0.01 us  [per_device(): face_all = lax.all_gather(face_packet, 'dom', axis=0)]
    dot_general x3, matrix products: 2.69 us -> 7.37 us  [per_device(): jnp.einsum('sdr,drq->sq', (wanted == cross_got[None]).astype(jnp.bfloat16...]
    dot_general x3, matrix products: 3.7 us -> 6.48 us  [per_device(): jnp.einsum('sdr,drq->sq', (wanted == inner_got[None]).astype(jnp.bfloat16...]
  transfers between devices with their start and end apart: 2 -> 2, of which waited for: 1 -> 0; matrix products, arithmetic and copies ran while one was open for 29% -> 30% of each run, Pallas kernels for 45% -> 50%
where the time goes in v6:
time: 163 us; the launch traced here: 160 us
  Pallas kernels  80.2 us (49%)
  matrix products  34.8 us (21%)
  other arithmetic  22.4 us (14%)
  between operations  14.6 us (9%)
  local copies, waits for them, and re-layouts  7.96 us (5%)
    pallas_call x4, Pallas kernels, direct_gather(): pl.pallas_call(kernel, out_shape=tuple((jax.ShapeDtypeStruct((n,) + x.sha...  80.2 us
    dot_general x3, matrix products, coarse_terms(): jnp.einsum('rci,rdi->rcd', row_side, products, preferred_element_type=jnp...  17.4 us
    dot_general x3, matrix products, per_device(): jnp.einsum('sdr,drq->sq', (wanted == cross_got[None]).astype(jnp.bfloat16...  7.37 us
    dot_general x3, matrix products, per_device(): jnp.einsum('sdr,drq->sq', (wanted == inner_got[None]).astype(jnp.bfloat16...  6.48 us
  transfers between devices with their start and end apart: 2, of which 0 were waited for; matrix products, arithmetic and copies ran while one was open for 30% of the time, Pallas kernels for 50%

profile of v6, /device:TPU:1, one launch (start us, length us, event | category | flops | bytes accessed | tf_op | source)
XLA Modules:
  0.0 160.1 jit_solution(1739663026729992139)
XLA Ops:
  7.7 4.3 %fusion.27 = bf16[16,48,48]{2,1,0:T(8,128)(2,1)S(1)} fusion(bf16[16,384,384]{2,1,0:T(8,128)(2,1)} %param.16, f32[48,384]{1,0:T(8,128)S(1)} %mul.217, f32[16,384]{1,0:T(8,128)} %x_ref.1), kind=kOutput, calls=%fused_computation.38 | convolution fusion | flops 256315392 | bytes 4890624 | tf_op jit(solution)/shard_map/rci,rdi->rcd/dot_general | solution.py:49
  12.0 0.9 convert_element_type.145
  13.4 0.4 fusion.58
  13.9 1.9 %broadcast_multiply_fusion = bf16[32,48,6,4,4,4]{1,0,5,4,3,2:T(8,128)(2,1)S(1)} fusion(f32[48,6,4,4,4]{0,4,3,2,1:T(4,128)S(1)} %broadcast_multiply_fusion.2, f32[32,6,4,4,4]{0,4,3,2,1:T(4,128)S(1)} %bitcast.75), kind=kLoop, calls=%fused_computation.21 | loop fusion | flops 1179648 | bytes 1302528 | tf_op jit(solution)/shard_map/mul | solution.py:21
  15.9 1.0 reverse_select_fusion.2
  17.0 14.3 %shard_map.131 = f32[16,16,384]{2,1,0:T(8,128)} custom-call(f32[16,384]{1,0:T(8,128)} %x_ref.1), custom_call_target="tpu_custom_call" | custom-call | tf_op jit(solution)/shard_map/pallas_call | solution.py:110
  31.2 1.3 fusion.56
  32.5 1.3 reverse_select_fusion.1
  33.8 1.1 fusion
  35.0 8.9 %fusion.18 = bf16[32,48,48]{2,1,0:T(8,128)(2,1)} fusion(bf16[32,384,384]{2,1,0:T(8,128)(2,1)} %param.17, bf16[32,48,384]{1,0,2:T(8,128)(2,1)S(1)} %bitcast.71, f32[48,384]{1,0:T(8,128)S(1)} %mul.217, f32[32,384]{1,0:T(8,128)S(1)} %fusion.56), kind=kOutput, calls=%fused_computation.30 | convolution fusion | flops 511451136 | bytes 10887168 | tf_op jit(solution)/shard_map/rci,rdi->rcd/dot_general | solution.py:49
  43.8 1.4 convert_element_type.153
  45.5 0.7 maximum_bitcast_fusion
  46.2 0.6 compare_reduce_fusion.1
  46.9 0.6 compare_reduce_fusion
  47.6 0.6 fusion.68
  48.3 0.6 broadcast_select_fusion
  49.1 0.6 pad_maximum_fusion.2.x_ref
  49.7 9.1 %shard_map.132 = f32[8,16,512]{2,1,0:T(8,128)} custom-call(f32[16,512]{1,0:T(8,128)} %pad_maximum_fusion.2.x_ref), custom_call_target="tpu_custom_call" | custom-call | tf_op jit(solution)/shard_map/pallas_call | solution.py:110
  58.9 1.1 convert_reduce_fusion
  60.0 1.1 fusion.55
  61.1 0.2 reduce_window_sum.11
  61.3 0.2 fusion.83
  61.5 0.2 select_reduce_fusion
  62.1 0.4 fusion.62
  62.5 1.2 broadcast_multiply_fusion.1
  63.7 0.6 reverse_select_fusion.5
  64.3 0.7 reverse_select_fusion.4
  65.0 0.7 fusion.4
  65.7 0.3 slice-done
  65.9 0.2 fusion.61
  66.2 4.3 %fusion.28 = bf16[16,48,48]{2,1,0:T(8,128)(2,1)S(1)} fusion(bf16[16,384,384]{2,1,0:T(8,128)(2,1)} %param.18, bf16[16,48,384]{1,0,2:T(8,128)(2,1)S(1)} %bitcast.72, f32[16,384]{1,0:T(8,128)S(1)} %fusion.61, f32[48,384]{1,0:T(8,128)S(1)} %mul.217), kind=kOutput, calls=%fused_computation.39 | convolution fusion | flops 255725568 | bytes 5480448 | tf_op jit(solution)/shard_map/rci,rdi->rcd/dot_general | solution.py:49
  70.4 0.8 convert_element_type.165.x_ref
  71.3 11.0 %shard_map.133 = bf16[8,16,2304]{2,1,0:T(8,128)(2,1)} custom-call(bf16[16,2304]{1,0:T(8,128)(2,1)} %convert_element_type.165.x_ref), custom_call_target="tpu_custom_call" | custom-call | tf_op jit(solution)/shard_map/pallas_call | solution.py:110
  82.3 1.3 convolution_convert_fusion
  83.7 0.7 pad_maximum_fusion.1.x_ref
  84.4 45.8 %shard_map.134 = bf16[16,25,2304]{2,1,0:T(8,128)(2,1)} custom-call(bf16[25,2304]{1,0:T(8,128)(2,1)} %pad_maximum_fusion.1.x_ref), custom_call_target="tpu_custom_call" | custom-call | tf_op jit(solution)/shard_map/pallas_call | solution.py:110
  130.2 1.1 slice.71
  131.6 4.1 %convolution_bitcast_fusion.2 = f32[256,2304]{1,0:T(8,128)} fusion(bf16[16,25,2304]{2,1,0:T(8,128)(2,1)} %shard_map.134, s32[16,25]{1,0:T(8,128)S(1)} %pad.24, s32[256]{0:T(256)S(1)} %iota_multiply_fusion), kind=kOutput, calls=%fused_computation.10 | convolution fusion | flops 471961600 | bytes 4205120 | tf_op jit(solution)/shard_map/sdr,drq->sq/dot_general | solution.py:232
  135.8 2.3 %convolution_bitcast_fusion.1 = f32[256,2304]{1,0:T(8,128)} fusion(bf16[16,25,2304]{2,1,0:T(8,128)(2,1)S(1)} %copy-done, s32[256]{0:T(256)S(1)} %fusion.67, s32[16,25]{1,0:T(8,128)S(1)} %pad.24), kind=kOutput, calls=%fused_computation.9 | convolution fusion | flops 471961600 | bytes 4205120 | tf_op jit(solution)/shard_map/sdr,drq->sq/dot_general | solution.py:232
  138.1 0.9 convolution_bitcast_fusion
  139.0 2.8 %bitcast_convert_fusion = f32[256,2304]{1,0:T(8,128)} fusion(bf16[16,16,2304]{2,1,0:T(8,128)(2,1)} %all-gather.5.cloned.1.call-done), kind=kLoop, calls=%fused_computation.33 | loop fusion | flops 589824 | bytes 3538944 | tf_op jit(solution)/shard_map/convert_element_type | solution.py:239
  141.9 1.1 slice.75
  143.2 0.1 slice.67
  143.4 4.0 %fusion.1 = f32[256,2304]{1,0:T(8,128)S(1)} fusion(f32[256,2304]{1,0:T(8,128)} %convolution_bitcast_fusion.2, bf16[16,33,2304]{2,1,0:T(8,128)(2,1)} %all-gather.7.cloned.1.call-done, s32[16,33]{1,0:T(8,128)S(1)} %pad.22, s32[256]{0:T(256)S(1)} %iota_multiply_fusion), kind=kOutput, calls=%fused_computation.14 | convolution fusion | flops 623579136 | bytes 7154752 | tf_op jit(solution)/shard_map/sdr,drq->sq/dot_general | solution.py:228
  147.4 0.1 copy-done.2
  147.5 1.2 fusion.2
  148.7 1.3 fusion.3
  150.0 3.2 %pad_maximum_fusion = f32[256,6912]{1,0:T(8,128)} fusion(f32[256,2304]{1,0:T(8,128)S(1)} %fusion.3, f32[256,2304]{1,0:T(8,128)S(1)} %fusion.2, f32[256,2304]{1,0:T(8,128)S(1)} %fusion.1), kind=kLoop, calls=%fused_computation.3 | loop fusion | flops 3538944 | bytes 14155776 | tf_op jit(solution)/shard_map/concatenate | solution.py:237
  (86 shorter events, 2.6 us)
Async XLA Ops:
  7.2 131.9 %all-gather.5.cloned.1.call-start = ((), (), s32[]{:S(2)}) async-start(), calls=%async_computation | async-start | bytes 1253376 | tf_op jit(solution)/shard_map/all_gather | solution.py:177
  7.7 5.7 %copy-start.3 = (f32[16,384]{1,0:T(8,128)S(1)}, f32[16,384]{1,0:T(8,128)}, u32[]{:S(2)}) copy-start(f32[16,384]{1,0:T(8,128)} %x_ref.1) | copy-start | bytes 73732
  7.7 5.7 %copy-start.5 = (s32[32]{0:T(128)S(1)}, s32[32]{0:T(128)}, u32[]{:S(2)}) copy-start(s32[32]{0:T(128)} %param.20) | copy-start | bytes 388
  7.7 6.1 %copy-start.9 = (s32[32]{0:T(128)S(1)}, s32[32]{0:T(128)}, u32[]{:S(2)}) copy-start(s32[32]{0:T(128)} %param.22) | copy-start | bytes 388
  12.9 129.0 %all-gather.7.cloned.1.call-start = ((), (), s32[]{:S(2)}) async-start(), calls=%async_computation.1 | async-start | bytes 3133440 | tf_op jit(solution)/shard_map/all_gather | solution.py:214
  15.8 1.1 copy-start.7
  15.9 1.1 copy-start.8
  34.9 12.6 %copy-start.11 = (s32[16,1]{0,1:T(1,128)S(1)}, s32[16,1]{0,1:T(1,128)}, u32[]{:S(2)}) copy-start(s32[16,1]{0,1:T(1,128)} %param.25) | copy-start | bytes 196
  34.9 12.7 %copy-start.12 = (s32[16]{0:T(128)S(1)}, s32[16]{0:T(128)}, u32[]{:S(2)}) copy-start(s32[16]{0:T(128)} %param.27) | copy-start | bytes 196
  34.9 14.2 %copy-start.4 = (f32[16,384]{1,0:T(8,128)S(1)}, f32[16,384]{1,0:T(8,128)}, u32[]{:S(2)}) copy-start(f32[16,384]{1,0:T(8,128)} %x_ref.1) | copy-start | bytes 73732
  35.0 27.2 %copy-start.6 = (s32[16]{0:T(128)S(1)}, s32[16]{0:T(128)}, u32[]{:S(2)}) copy-start(s32[16]{0:T(128)} %param.21) | copy-start | bytes 196
  43.8 19.8 %copy-start.10 = (s32[16]{0:T(128)S(1)}, s32[16]{0:T(128)}, u32[]{:S(2)}) copy-start(s32[16]{0:T(128)} %param.23) | copy-start | bytes 196
  65.0 0.9 slice-start
  131.6 4.2 %copy-start = (bf16[16,25,2304]{2,1,0:T(8,128)(2,1)S(1)}, bf16[16,25,2304]{2,1,0:T(8,128)(2,1)}, u32[]{:S(2)}) copy-start(bf16[16,25,2304]{2,1,0:T(8,128)(2,1)} %shard_map.134) | copy-start | bytes 5529604
  143.4 4.0 %copy-start.1 = (bf16[16,33,2304]{2,1,0:T(8,128)(2,1)S(1)}, bf16[16,33,2304]{2,1,0:T(8,128)(2,1)}, u32[]{:S(2)}) copy-start(bf16[16,33,2304]{2,1,0:T(8,128)(2,1)} %all-gather.7.cloned.1.call-done) | copy-start | bytes 7299076
  143.4 4.1 %copy-start.2 = (f32[256,2304]{1,0:T(8,128)S(1)}, f32[256,2304]{1,0:T(8,128)}, u32[]{:S(2)}) copy-start(f32[256,2304]{1,0:T(8,128)} %convolution_bitcast_fusion.1) | copy-start | bytes 7077892
Sparse Core Ops, SparseCore 0:
  13.0 44.7 all-gather.4
  60.0 70.5 all-gather.6

commit v7 on v5

--- a/solution.py
+++ b/solution.py
@@ -49,15 +49,16 @@
     return jnp.einsum("rci,rdi->rcd", row_side, products, preferred_element_type=jnp.float32)
 
 
-def direct_gather(x, axes, order, collective_id):
+def direct_gather(xs, axes, order, collective_id):
     sizes = [lax.axis_size(axis) for axis in axes]
 
     def device(axis, peer):
         return tuple(peer if name == axis else lax.axis_index(name) for name in order)
 
-    def kernel(x_ref, *rest):
-        outs = rest[: len(axes)]
-        send_sem, recv_sem, local_sem = rest[len(axes):]
+    def kernel(*refs):
+        x_refs = refs[: len(axes)]
+        outs = refs[len(axes) : 2 * len(axes)]
+        send_sem, recv_sem, local_sem = refs[2 * len(axes) :]
         barrier = pltpu.get_barrier_semaphore()
         for axis, n in zip(axes, sizes):
             me = lax.axis_index(axis)
@@ -72,6 +73,7 @@
         base = 0
         for a, (axis, n) in enumerate(zip(axes, sizes)):
             me = lax.axis_index(axis)
+            x_ref = x_refs[a]
             local = pltpu.make_async_copy(x_ref, outs[a].at[me], local_sem.at[a])
             local.start()
             locals_.append(local)
@@ -95,7 +97,7 @@
             for step in range(1, n):
                 source = lax.rem(me - step + n, n)
                 pltpu.make_async_remote_copy(
-                    src_ref=x_ref,
+                    src_ref=x_refs[a],
                     dst_ref=outs[a].at[source],
                     send_sem=send_sem.at[base + step],
                     recv_sem=recv_sem.at[base + step],
@@ -109,8 +111,10 @@
     total = sum(sizes)
     return pl.pallas_call(
         kernel,
-        out_shape=tuple(jax.ShapeDtypeStruct((n,) + x.shape, x.dtype) for n in sizes),
-        in_specs=[pl.BlockSpec(memory_space=pl.ANY)],
+        out_shape=tuple(
+            jax.ShapeDtypeStruct((n,) + x.shape, x.dtype) for n, x in zip(sizes, xs)
+        ),
+        in_specs=[pl.BlockSpec(memory_space=pl.ANY) for _ in sizes],
         out_specs=tuple(pl.BlockSpec(memory_space=pl.ANY) for _ in sizes),
         scratch_shapes=[
             pltpu.SemaphoreType.DMA((total,)),
@@ -120,7 +124,7 @@
         compiler_params=pltpu.CompilerParams(
             collective_id=collective_id, has_side_effects=True
         ),
-    )(x)
+    )(*xs)
 
 
 def id_row(values, width):
@@ -161,7 +165,7 @@
     id_cols = id_cols.at[:cross_count, 1].set(target_cross.astype(jnp.float32))
     metric_ids = jnp.concatenate((metric, id_cols), axis=1)
     fine = metric.shape[1]
-    dom_got, grp_got = direct_gather(metric_ids, ("dom", "grp"), order, 0)
+    dom_got, grp_got = direct_gather((metric, metric_ids), ("dom", "grp"), order, 0)
     metric_dom = dom_got[:, :, :fine].reshape(-1, fine)
     metric_grp = grp_got[:, :, :fine].reshape(-1, fine)
     got_peer = grp_got[:, :cross_count, fine].astype(jnp.int32)
@@ -193,7 +197,7 @@
         pick_rows(peer_x * elem_count + target_cross // 3, metric_grp)
     )
     cross_c = coarse_terms(cross_row_side, cross_y).reshape(cross_count, square)
-    (got_rows,) = direct_gather(cross_c.astype(jnp.bfloat16), ("grp",), order, 1)
+    (got_rows,) = direct_gather((cross_c.astype(jnp.bfloat16),), ("grp",), order, 1)
     mine_rows = jnp.einsum(
         "skr,srq->skq", picks.astype(jnp.bfloat16), got_rows, preferred_element_type=jnp.float32
     ).astype(jnp.bfloat16).reshape(group_count * CROSS_CAP, square)
@@ -208,7 +212,7 @@
         (inner_c.astype(jnp.bfloat16), id_row(slot_code, square)), axis=0
     )
     face_all = lax.all_gather(face_packet, "dom", axis=0)
-    (cross_all,) = direct_gather(mine_rows, ("dom",), order, 2)
+    (cross_all,) = direct_gather((mine_rows,), ("dom",), order, 2)
     contrib_count = slots.shape[0]
     codes = face_all[:, inner_count, : 2 * contrib_count].astype(jnp.int32)
     got_slot = jnp.where(codes[:, 0::2] >= 0, codes[:, 0::2] * 32 + codes[:, 1::2], -1)

time: 141 us -> 140 us (level)
  Pallas kernels: 62.8 us -> 60.1 us
  waiting for transfers between devices: 5.49 us -> 7.37 us
    pallas_call x3, Pallas kernels: 62.8 us -> 60.1 us  [direct_gather(): pl.pallas_call(kernel, out_shape=tuple((jax.ShapeDtypeStruct((n,) + x.sha...]
    all_gather x1, waiting for transfers between devices: 5.44 us -> 7.31 us  [per_device(): face_all = lax.all_gather(face_packet, 'dom', axis=0)]
  transfers between devices with their start and end apart: 2 -> 2, of which waited for: 1 -> 1; matrix products, arithmetic and copies ran while one was open for 29% -> 28% of each run, Pallas kernels for 45% -> 43%
where the time goes in v7:
time: 140 us; the launch traced here: 139 us
  Pallas kernels  60.1 us (43%)
  matrix products  26.3 us (19%)
  other arithmetic  23.2 us (17%)
  between operations  14.5 us (10%)
  local copies, waits for them, and re-layouts  7.49 us (5%)
  waiting for transfers between devices  7.37 us (5%)
    pallas_call x3, Pallas kernels, direct_gather(): pl.pallas_call(kernel, out_shape=tuple((jax.ShapeDtypeStruct((n,) + x.sha...  60.1 us
    dot_general x3, matrix products, coarse_terms(): jnp.einsum('rci,rdi->rcd', row_side, products, preferred_element_type=jnp...  17.4 us
    all_gather x1, waiting for transfers between devices, per_device(): face_all = lax.all_gather(face_packet, 'dom', axis=0)  7.31 us
    dot_general x3, matrix products, per_device(): jnp.einsum('sdr,drq->sq', (wanted == inner_got[None]).astype(jnp.bfloat16...  3.7 us
    concatenate x1, other arithmetic, per_device(): face = jnp.concatenate(faces, axis=1)  3.21 us
    mul x2, other arithmetic, restrictor(): full = weights[:, None, :] * table[None]  3.1 us
    convert_element_type x1, other arithmetic, per_device(): diag_all[:, :elem_count, :].reshape(-1, square).astype(jnp.float32)  2.97 us
  transfers between devices with their start and end apart: 2, of which 1 were waited for; matrix products, arithmetic and copies ran while one was open for 28% of the time, Pallas kernels for 43%

profile of v7, /device:TPU:1, one launch (start us, length us, event | category | flops | bytes accessed | tf_op | source)
XLA Modules:
  0.0 139.1 jit_solution(2528559522249931849)
XLA Ops:
  7.8 4.3 %fusion.27 = bf16[16,48,48]{2,1,0:T(8,128)(2,1)S(1)} fusion(bf16[16,384,384]{2,1,0:T(8,128)(2,1)} %param.16, f32[48,384]{1,0:T(8,128)S(1)} %mul.211, f32[16,384]{1,0:T(8,128)} %refs_0_.1), kind=kOutput, calls=%fused_computation.38 | convolution fusion | flops 256315392 | bytes 4890624 | tf_op jit(solution)/shard_map/rci,rdi->rcd/dot_general | solution.py:49
  12.1 0.9 convert_element_type.139
  13.0 0.6 compare_reduce_fusion.1
  13.7 0.6 compare_reduce_fusion
  14.6 0.6 fusion.68
  15.3 0.6 broadcast_select_fusion
  16.1 0.6 pad_maximum_fusion.1.refs_1_
  16.7 14.8 %shard_map.131 = (f32[16,16,384]{2,1,0:T(8,128)}, f32[8,16,512]{2,1,0:T(8,128)}) custom-call(f32[16,384]{1,0:T(8,128)} %refs_0_.1, f32[16,512]{1,0:T(8,128)} %pad_maximum_fusion.1.refs_1_), custom_call_target="tpu_custom_call" | custom-call | tf_op jit(solution)/shard_map/pallas_call | solution.py:112
  31.5 1.1 convert_reduce_fusion
  32.7 1.1 fusion.55
  33.7 0.2 reduce_window_sum.11
  33.9 0.2 fusion.83
  34.1 0.2 select_reduce_fusion
  35.2 0.4 fusion.58
  35.6 1.9 %broadcast_multiply_fusion = bf16[32,48,6,4,4,4]{1,0,5,4,3,2:T(8,128)(2,1)S(1)} fusion(f32[48,6,4,4,4]{0,4,3,2,1:T(4,128)S(1)} %broadcast_multiply_fusion.2, f32[32,6,4,4,4]{0,4,3,2,1:T(4,128)S(1)} %bitcast.64), kind=kLoop, calls=%fused_computation.21 | loop fusion | flops 1179648 | bytes 1302528 | tf_op jit(solution)/shard_map/mul | solution.py:21
  37.6 0.3 fusion.56
  37.9 1.3 reverse_select_fusion.2
  39.2 1.5 %reverse_select_fusion.1 = bf16[32,48,6,4,4,4]{1,0,5,4,3,2:T(8,128)(2,1)S(1)} fusion(bf16[32,48,6,4,4,4]{1,0,5,4,3,2:T(8,128)(2,1)S(1)} %reverse_select_fusion.2, pred[32]{0:T(512)(128)(4,1)S(1)} %get-tuple-element.35), kind=kLoop, calls=%fused_computation.1 | loop fusion | flops 589824 | bytes 2359328 | tf_op jit(solution)/shard_map/jit(_where)/select_n | solution.py:25
  40.7 1.1 fusion
  41.9 8.9 %fusion.18 = bf16[32,48,48]{2,1,0:T(8,128)(2,1)} fusion(bf16[32,384,384]{2,1,0:T(8,128)(2,1)} %param.17, bf16[32,48,384]{1,0,2:T(8,128)(2,1)S(1)} %bitcast.62, f32[48,384]{1,0:T(8,128)S(1)} %mul.211, f32[32,384]{1,0:T(8,128)S(1)} %fusion.56), kind=kOutput, calls=%fused_computation.30 | convolution fusion | flops 511451136 | bytes 10887168 | tf_op jit(solution)/shard_map/rci,rdi->rcd/dot_general | solution.py:49
  50.7 1.4 convert_element_type.149
  52.1 0.7 maximum_bitcast_fusion
  52.8 0.9 slice.62
  53.8 0.4 fusion.62
  54.2 0.2 fusion.61
  54.4 1.2 broadcast_multiply_fusion.1
  55.6 0.6 reverse_select_fusion.5
  56.2 0.7 reverse_select_fusion.4
  56.9 0.7 fusion.4
  57.6 4.3 %fusion.28 = bf16[16,48,48]{2,1,0:T(8,128)(2,1)S(1)} fusion(bf16[16,384,384]{2,1,0:T(8,128)(2,1)} %param.18, bf16[16,48,384]{1,0,2:T(8,128)(2,1)S(1)} %bitcast.63, f32[16,384]{1,0:T(8,128)S(1)} %fusion.61, f32[48,384]{1,0:T(8,128)S(1)} %mul.211), kind=kOutput, calls=%fused_computation.39 | convolution fusion | flops 255725568 | bytes 5480448 | tf_op jit(solution)/shard_map/rci,rdi->rcd/dot_general | solution.py:49
  61.8 0.8 convert_element_type.162.refs_0_
  62.7 11.9 %shard_map.132 = bf16[8,16,2304]{2,1,0:T(8,128)(2,1)} custom-call(bf16[16,2304]{1,0:T(8,128)(2,1)} %convert_element_type.162.refs_0_), custom_call_target="tpu_custom_call" | custom-call | tf_op jit(solution)/shard_map/pallas_call | solution.py:112
  74.6 1.3 convolution_convert_fusion
  75.9 0.7 reshape.595.refs_0_
  76.6 33.4 %shard_map.133 = bf16[16,24,2304]{2,1,0:T(8,128)(2,1)} custom-call(bf16[24,2304]{1,0:T(8,128)(2,1)} %reshape.595.refs_0_), custom_call_target="tpu_custom_call" | custom-call | tf_op jit(solution)/shard_map/pallas_call | solution.py:112
  110.1 3.0 %bitcast_convert_fusion = f32[256,2304]{1,0:T(8,128)} fusion(bf16[16,16,2304]{2,1,0:T(8,128)(2,1)} %all-gather.5.cloned.1.call-done), kind=kLoop, calls=%fused_computation.33 | loop fusion | flops 589824 | bytes 3538944 | tf_op jit(solution)/shard_map/convert_element_type | solution.py:236
  113.1 7.3 %all-gather.7.cloned.1.call-done = bf16[16,33,2304]{2,1,0:T(8,128)(2,1)} async-done(((bf16[1,33,2304]{2,1,0:T(8,128)(2,1)}), bf16[16,33,2304]{2,1,0:T(8,128)(2,1)}) %all-gather.7.cloned.1.call-update) | async-done | bytes 2433040 | tf_op jit(solution)/shard_map/all_gather | solution.py:214
  120.4 0.8 slice_convert_fusion
  121.2 0.2 slice.58
  121.4 0.2 slice.59
  121.7 0.9 convolution_bitcast_fusion.2
  122.6 0.9 convolution_bitcast_fusion.1
  123.5 0.9 convolution_bitcast_fusion
  124.4 0.9 copy-done.1
  125.3 1.2 fusion.1
  126.5 1.2 fusion.2
  127.8 1.2 fusion.3
  129.0 3.2 %pad_maximum_fusion = f32[256,6912]{1,0:T(8,128)} fusion(f32[256,2304]{1,0:T(8,128)S(1)} %fusion.3, f32[256,2304]{1,0:T(8,128)S(1)} %fusion.2, f32[256,2304]{1,0:T(8,128)S(1)} %fusion.1), kind=kLoop, calls=%fused_computation.3 | loop fusion | flops 3538944 | bytes 14155776 | tf_op jit(solution)/shard_map/concatenate | solution.py:234
  (72 shorter events, 2.1 us)
Async XLA Ops:
  7.2 103.0 %all-gather.5.cloned.1.call-start = ((), (), s32[]{:S(2)}) async-start(), calls=%async_computation | async-start | bytes 1253376 | tf_op jit(solution)/shard_map/all_gather | solution.py:193
  7.7 6.8 %copy-start.12 = (s32[16,1]{0,1:T(1,128)S(1)}, s32[16,1]{0,1:T(1,128)}, u32[]{:S(2)}) copy-start(s32[16,1]{0,1:T(1,128)} %param.25) | copy-start | bytes 196
  7.7 6.9 %copy-start.13 = (s32[16]{0:T(128)S(1)}, s32[16]{0:T(128)}, u32[]{:S(2)}) copy-start(s32[16]{0:T(128)} %param.27) | copy-start | bytes 196
  7.7 8.4 %copy-start.2 = (f32[16,384]{1,0:T(8,128)S(1)}, f32[16,384]{1,0:T(8,128)}, u32[]{:S(2)}) copy-start(f32[16,384]{1,0:T(8,128)} %refs_0_.1) | copy-start | bytes 73732
  7.7 26.7 %copy-start.8 = (s32[32]{0:T(128)S(1)}, s32[32]{0:T(128)}, u32[]{:S(2)}) copy-start(s32[32]{0:T(128)} %param.26) | copy-start | bytes 388
  7.8 26.7 %copy-start.9 = (s32[32,1]{0,1:T(1,128)S(1)}, s32[32,1]{0,1:T(1,128)}, u32[]{:S(2)}) copy-start(s32[32,1]{0,1:T(1,128)} %param.24) | copy-start | bytes 388
  7.8 27.4 %copy-start.3 = (f32[16,384]{1,0:T(8,128)S(1)}, f32[16,384]{1,0:T(8,128)}, u32[]{:S(2)}) copy-start(f32[16,384]{1,0:T(8,128)} %refs_0_.1) | copy-start | bytes 73732
  7.8 27.4 %copy-start.5 = (s32[32]{0:T(128)S(1)}, s32[32]{0:T(128)}, u32[]{:S(2)}) copy-start(s32[32]{0:T(128)} %param.20) | copy-start | bytes 388
  7.8 27.8 %copy-start.10 = (s32[32]{0:T(128)S(1)}, s32[32]{0:T(128)}, u32[]{:S(2)}) copy-start(s32[32]{0:T(128)} %param.22) | copy-start | bytes 388
  13.0 107.4 %all-gather.7.cloned.1.call-start = ((), (), s32[]{:S(2)}) async-start(), calls=%async_computation.1 | async-start | bytes 3133440 | tf_op jit(solution)/shard_map/all_gather | solution.py:214
  34.4 3.2 %copy-start.4 = (f32[16,16,384]{2,1,0:T(8,128)S(1)}, f32[16,16,384]{2,1,0:T(8,128)}, u32[]{:S(2)}) copy-start(f32[16,16,384]{2,1,0:T(8,128)} %get-tuple-element.28) | copy-start | bytes 1179652
  41.8 11.9 %copy-start.11 = (s32[16]{0:T(128)S(1)}, s32[16]{0:T(128)}, u32[]{:S(2)}) copy-start(s32[16]{0:T(128)} %param.23) | copy-start | bytes 196
  41.9 12.0 %copy-start.6 = (s32[16]{0:T(128)S(1)}, s32[16]{0:T(128)}, u32[]{:S(2)}) copy-start(s32[16]{0:T(128)} %param.21) | copy-start | bytes 196
  76.6 45.0 %copy-start.7 = (pred[33]{0:T(512)(128)(4,1)S(1)}, pred[33]{0:T(512)(128)(4,1)}, u32[]{:S(2)}) copy-start(pred[33]{0:T(512)(128)(4,1)} %constant.205.clone.1) | copy-start | bytes 103
  110.1 11.6 %copy-start = (bf16[16,24,2304]{2,1,0:T(8,128)(2,1)S(1)}, bf16[16,24,2304]{2,1,0:T(8,128)(2,1)}, u32[]{:S(2)}) copy-start(bf16[16,24,2304]{2,1,0:T(8,128)(2,1)} %shard_map.133) | copy-start | bytes 5308420
  123.5 1.8 %copy-start.1 = (bf16[16,33,2304]{2,1,0:T(8,128)(2,1)S(1)}, bf16[16,33,2304]{2,1,0:T(8,128)(2,1)}, u32[]{:S(2)}) copy-start(bf16[16,33,2304]{2,1,0:T(8,128)(2,1)} %all-gather.7.cloned.1.call-done) | copy-start | bytes 7299076
Sparse Core Ops, SparseCore 0:
  13.1 44.5 all-gather.4
  60.4 59.9 all-gather.6

commit v8 on v7

--- a/solution.py
+++ b/solution.py
@@ -127,12 +127,22 @@
     )(*xs)
 
 
+def slot_codes(slots):
+    valid = slots >= 0
+    return jnp.stack((jnp.where(valid, slots // 32, -1), jnp.where(valid, slots % 32, 0)), axis=1)
+
+
+def read_codes(row, count):
+    codes = row[:, : 2 * count].astype(jnp.int32)
+    return jnp.where(codes[:, 0::2] >= 0, codes[:, 0::2] * 32 + codes[:, 1::2], -1)
+
+
 def id_row(values, width):
     flat = values.reshape(-1).astype(jnp.bfloat16)
     return jnp.pad(flat, (0, width - flat.shape[0]))[None, :]
 
 
-def per_device(
+def device_body(
     diag_blocks,
     face_in,
     face_cross,
@@ -181,11 +191,6 @@
         jnp.any(picks, axis=2), my_dom * slots_dev + mine_target, -1
     ).reshape(-1)
     inner_slot = peer_i * slots_dev + target_in
-    slots = jnp.concatenate((inner_slot, mine_slot), axis=0)
-    valid = slots >= 0
-    slot_code = jnp.stack(
-        (jnp.where(valid, slots // 32, -1), jnp.where(valid, slots % 32, 0)), axis=1
-    )
 
     diag_side = plain_restrictor(metric)
     diag_c = coarse_terms(diag_side, one_sided(diag_blocks, diag_side))
@@ -209,15 +214,18 @@
     inner_c = coarse_terms(inner_row_side, inner_y).reshape(inner_count, square)
 
     face_packet = jnp.concatenate(
-        (inner_c.astype(jnp.bfloat16), id_row(slot_code, square)), axis=0
+        (inner_c.astype(jnp.bfloat16), id_row(slot_codes(inner_slot), square)), axis=0
     )
     face_all = lax.all_gather(face_packet, "dom", axis=0)
-    (cross_all,) = direct_gather((mine_rows,), ("dom",), order, 2)
-    contrib_count = slots.shape[0]
-    codes = face_all[:, inner_count, : 2 * contrib_count].astype(jnp.int32)
-    got_slot = jnp.where(codes[:, 0::2] >= 0, codes[:, 0::2] * 32 + codes[:, 1::2], -1)
-    inner_got = jnp.pad(got_slot[:, :inner_count], ((0, 0), (0, 1)), constant_values=-1)
-    cross_got = got_slot[:, inner_count:]
+    cross_packet = jnp.concatenate((mine_rows, id_row(slot_codes(mine_slot), square)), axis=0)
+    (cross_all,) = direct_gather((cross_packet,), ("dom",), order, 2)
+    inner_got = jnp.pad(
+        read_codes(face_all[:, inner_count], inner_count), ((0, 0), (0, 1)), constant_values=-1
+    )
+    cross_got = jnp.pad(
+        read_codes(cross_all[:, mine_rows.shape[0]], mine_rows.shape[0]),
+        ((0, 0), (0, 1)), constant_values=-1,
+    )
     group_elems = group_width * elem_count
     faces = []
     for slot in range(3):
@@ -254,7 +262,7 @@
         P(("grp", "dom")),
     )
     return jax.shard_map(
-        per_device,
+        device_body,
         mesh=mesh,
         in_specs=placed,
         out_specs=(P("grp", None), P("grp", None)),

time: 140 us -> 157 us (1.12)
  Pallas kernels: 60.1 us -> 75.6 us
  matrix products: 26.3 us -> 34.8 us
  waiting for transfers between devices: 7.37 us -> 0.06 us
    pallas_call x3, Pallas kernels: 60.1 us -> 75.6 us  [direct_gather(): pl.pallas_call(kernel, out_shape=tuple((jax.ShapeDtypeStruct((n,) + x.sha...]
    dot_general x7, matrix products: 7.67 us -> 15.1 us  [the longest x3 7.37 us: device_body(): jnp.einsum('sdr,drq->sq', (wanted == cross_got[None]).astype(jnp.bfloat16...]
    all_gather x2, waiting for transfers between devices: 7.33 us -> 0.02 us  [the longest x1 0.02 us: device_body(): diag_all = lax.all_gather(diag_rows, 'dom', axis=0)]
    slice x4 -> x7, local copies, waits for them, and re-layouts: 1.38 us -> 3.73 us  [the longest x1 1.15 us: device_body(): cross_all[:, mine_rows.shape[0]]]
    convert_element_type x5 -> x6, other arithmetic: 4.87 us -> 3.97 us  [the longest x1 2.83 us: device_body(): diag_all[:, :elem_count, :].reshape(-1, square).astype(jnp.float32)]
    concatenate x2 -> x3, other arithmetic: 3.83 us -> 4.51 us  [the longest x1 3.21 us: device_body(): face = jnp.concatenate(faces, axis=1)]
  transfers between devices with their start and end apart: 2 -> 2, of which waited for: 1 -> 0; matrix products, arithmetic and copies ran while one was open for 28% -> 31% of each run, Pallas kernels for 43% -> 48%
where the time goes in v8:
time: 157 us; the launch traced here: 156 us
  Pallas kernels  75.6 us (48%)
  matrix products  34.8 us (22%)
  other arithmetic  22.4 us (14%)
  between operations  14.6 us (9%)
  local copies, waits for them, and re-layouts  8.78 us (6%)
    pallas_call x3, Pallas kernels, direct_gather(): pl.pallas_call(kernel, out_shape=tuple((jax.ShapeDtypeStruct((n,) + x.sha...  75.6 us
    dot_general x3, matrix products, coarse_terms(): jnp.einsum('rci,rdi->rcd', row_side, products, preferred_element_type=jnp...  17.4 us
    dot_general x3, matrix products, device_body(): jnp.einsum('sdr,drq->sq', (wanted == cross_got[None]).astype(jnp.bfloat16...  7.37 us
    dot_general x3, matrix products, device_body(): jnp.einsum('sdr,drq->sq', (wanted == inner_got[None]).astype(jnp.bfloat16...  6.48 us
    concatenate x1, other arithmetic, device_body(): face = jnp.concatenate(faces, axis=1)  3.21 us
    mul x2, other arithmetic, restrictor(): full = weights[:, None, :] * table[None]  3.15 us
  transfers between devices with their start and end apart: 2, of which 0 were waited for; matrix products, arithmetic and copies ran while one was open for 31% of the time, Pallas kernels for 48%

profile of v8, /device:TPU:1, one launch (start us, length us, event | category | flops | bytes accessed | tf_op | source)
XLA Modules:
  0.0 156.4 jit_solution(16032409269542371457)
XLA Ops:
  7.8 4.3 %fusion.27 = bf16[16,48,48]{2,1,0:T(8,128)(2,1)S(1)} fusion(bf16[16,384,384]{2,1,0:T(8,128)(2,1)} %param.16, f32[48,384]{1,0:T(8,128)S(1)} %mul.217, f32[16,384]{1,0:T(8,128)} %refs_0_.1), kind=kOutput, calls=%fused_computation.38 | convolution fusion | flops 256315392 | bytes 4890624 | tf_op jit(solution)/shard_map/rci,rdi->rcd/dot_general | solution.py:49
  12.1 0.8 convert_element_type.145
  13.0 0.6 compare_reduce_fusion.1
  13.6 0.6 compare_reduce_fusion
  14.5 0.6 fusion.68
  15.6 0.4 fusion.58
  16.0 0.7 broadcast_select_fusion
  16.7 1.9 %broadcast_multiply_fusion = bf16[32,48,6,4,4,4]{1,0,5,4,3,2:T(8,128)(2,1)S(1)} fusion(f32[48,6,4,4,4]{0,4,3,2,1:T(4,128)S(1)} %broadcast_multiply_fusion.2, f32[32,6,4,4,4]{0,4,3,2,1:T(4,128)S(1)} %bitcast.73), kind=kLoop, calls=%fused_computation.21 | loop fusion | flops 1179648 | bytes 1302528 | tf_op jit(solution)/shard_map/mul | solution.py:21
  18.7 1.0 reverse_select_fusion.2
  19.8 0.3 scatter.9
  20.0 0.6 pad_maximum_fusion.2.refs_1_
  20.7 14.8 %shard_map.131 = (f32[16,16,384]{2,1,0:T(8,128)}, f32[8,16,512]{2,1,0:T(8,128)}) custom-call(f32[16,384]{1,0:T(8,128)} %refs_0_.1, f32[16,512]{1,0:T(8,128)} %pad_maximum_fusion.2.refs_1_), custom_call_target="tpu_custom_call" | custom-call | tf_op jit(solution)/shard_map/pallas_call | solution.py:112
  35.4 1.3 fusion.56
  36.7 1.3 reverse_select_fusion.1
  38.0 1.1 fusion
  39.2 8.9 %fusion.18 = bf16[32,48,48]{2,1,0:T(8,128)(2,1)} fusion(bf16[32,384,384]{2,1,0:T(8,128)(2,1)} %param.17, bf16[32,48,384]{1,0,2:T(8,128)(2,1)S(1)} %bitcast.71, f32[48,384]{1,0:T(8,128)S(1)} %mul.217, f32[32,384]{1,0:T(8,128)S(1)} %fusion.56), kind=kOutput, calls=%fused_computation.30 | convolution fusion | flops 511451136 | bytes 10887168 | tf_op jit(solution)/shard_map/rci,rdi->rcd/dot_general | solution.py:49
  48.0 1.4 convert_element_type.155
  49.7 0.7 maximum_bitcast_fusion
  50.4 1.1 convert_reduce_fusion
  51.5 0.9 slice.69
  52.5 1.1 fusion.55
  53.6 0.2 reduce_window_sum.11
  53.7 0.2 fusion.83
  54.0 0.2 select_reduce_fusion
  54.6 0.4 fusion.62
  54.9 1.2 broadcast_multiply_fusion.1
  56.2 0.6 reverse_select_fusion.5
  56.8 0.7 reverse_select_fusion.4
  57.5 0.7 fusion.4
  58.2 0.2 fusion.61
  58.4 4.3 %fusion.28 = bf16[16,48,48]{2,1,0:T(8,128)(2,1)S(1)} fusion(bf16[16,384,384]{2,1,0:T(8,128)(2,1)} %param.18, bf16[16,48,384]{1,0,2:T(8,128)(2,1)S(1)} %bitcast.72, f32[16,384]{1,0:T(8,128)S(1)} %fusion.61, f32[48,384]{1,0:T(8,128)S(1)} %mul.217), kind=kOutput, calls=%fused_computation.39 | convolution fusion | flops 255725568 | bytes 5480448 | tf_op jit(solution)/shard_map/rci,rdi->rcd/dot_general | solution.py:49
  62.7 0.8 convert_element_type.165.refs_0_
  63.5 12.2 %shard_map.132 = bf16[8,16,2304]{2,1,0:T(8,128)(2,1)} custom-call(bf16[16,2304]{1,0:T(8,128)(2,1)} %convert_element_type.165.refs_0_), custom_call_target="tpu_custom_call" | custom-call | tf_op jit(solution)/shard_map/pallas_call | solution.py:112
  75.7 1.3 convolution_convert_fusion
  77.1 0.7 pad_maximum_fusion.1.refs_0_
  77.8 48.7 %shard_map.133 = bf16[16,25,2304]{2,1,0:T(8,128)(2,1)} custom-call(bf16[25,2304]{1,0:T(8,128)(2,1)} %pad_maximum_fusion.1.refs_0_), custom_call_target="tpu_custom_call" | custom-call | tf_op jit(solution)/shard_map/pallas_call | solution.py:112
  126.5 1.1 slice.71
  128.0 4.2 %convolution_bitcast_fusion.2 = f32[256,2304]{1,0:T(8,128)} fusion(bf16[16,25,2304]{2,1,0:T(8,128)(2,1)} %shard_map.133, s32[16,25]{1,0:T(8,128)S(1)} %pad.24, s32[256]{0:T(256)S(1)} %iota_multiply_fusion), kind=kOutput, calls=%fused_computation.10 | convolution fusion | flops 471961600 | bytes 4205120 | tf_op jit(solution)/shard_map/sdr,drq->sq/dot_general | solution.py:237
  132.1 2.3 %convolution_bitcast_fusion.1 = f32[256,2304]{1,0:T(8,128)} fusion(bf16[16,25,2304]{2,1,0:T(8,128)(2,1)S(1)} %copy-done, s32[256]{0:T(256)S(1)} %fusion.67, s32[16,25]{1,0:T(8,128)S(1)} %pad.24), kind=kOutput, calls=%fused_computation.9 | convolution fusion | flops 471961600 | bytes 4205120 | tf_op jit(solution)/shard_map/sdr,drq->sq/dot_general | solution.py:237
  134.4 0.9 convolution_bitcast_fusion
  135.4 2.8 %bitcast_convert_fusion = f32[256,2304]{1,0:T(8,128)} fusion(bf16[16,16,2304]{2,1,0:T(8,128)(2,1)} %all-gather.5.cloned.1.call-done), kind=kLoop, calls=%fused_computation.33 | loop fusion | flops 589824 | bytes 3538944 | tf_op jit(solution)/shard_map/convert_element_type | solution.py:244
  138.2 1.1 slice.75
  139.5 0.1 slice.67
  139.7 4.0 %fusion.1 = f32[256,2304]{1,0:T(8,128)S(1)} fusion(f32[256,2304]{1,0:T(8,128)} %convolution_bitcast_fusion.2, bf16[16,33,2304]{2,1,0:T(8,128)(2,1)} %all-gather.7.cloned.1.call-done, s32[16,33]{1,0:T(8,128)S(1)} %pad.22, s32[256]{0:T(256)S(1)} %iota_multiply_fusion), kind=kOutput, calls=%fused_computation.14 | convolution fusion | flops 623579136 | bytes 7154752 | tf_op jit(solution)/shard_map/sdr,drq->sq/dot_general | solution.py:233
  143.7 0.1 copy-done.2
  143.8 1.2 fusion.2
  145.1 1.3 fusion.3
  146.4 3.2 %pad_maximum_fusion = f32[256,6912]{1,0:T(8,128)} fusion(f32[256,2304]{1,0:T(8,128)S(1)} %fusion.3, f32[256,2304]{1,0:T(8,128)S(1)} %fusion.2, f32[256,2304]{1,0:T(8,128)S(1)} %fusion.1), kind=kLoop, calls=%fused_computation.3 | loop fusion | flops 3538944 | bytes 14155776 | tf_op jit(solution)/shard_map/concatenate | solution.py:242
  (84 shorter events, 2.5 us)
Async XLA Ops:
  7.2 128.2 %all-gather.5.cloned.1.call-start = ((), (), s32[]{:S(2)}) async-start(), calls=%async_computation | async-start | bytes 1253376 | tf_op jit(solution)/shard_map/all_gather | solution.py:198
  7.7 6.7 %copy-start.11 = (s32[16,1]{0,1:T(1,128)S(1)}, s32[16,1]{0,1:T(1,128)}, u32[]{:S(2)}) copy-start(s32[16,1]{0,1:T(1,128)} %param.25) | copy-start | bytes 196
  7.7 6.8 %copy-start.12 = (s32[16]{0:T(128)S(1)}, s32[16]{0:T(128)}, u32[]{:S(2)}) copy-start(s32[16]{0:T(128)} %param.27) | copy-start | bytes 196
  7.7 7.8 %copy-start.3 = (f32[16,384]{1,0:T(8,128)S(1)}, f32[16,384]{1,0:T(8,128)}, u32[]{:S(2)}) copy-start(f32[16,384]{1,0:T(8,128)} %refs_0_.1) | copy-start | bytes 73732
  7.7 7.8 %copy-start.5 = (s32[32]{0:T(128)S(1)}, s32[32]{0:T(128)}, u32[]{:S(2)}) copy-start(s32[32]{0:T(128)} %param.20) | copy-start | bytes 388
  7.8 8.2 %copy-start.9 = (s32[32]{0:T(128)S(1)}, s32[32]{0:T(128)}, u32[]{:S(2)}) copy-start(s32[32]{0:T(128)} %param.22) | copy-start | bytes 388
  12.9 125.3 %all-gather.7.cloned.1.call-start = ((), (), s32[]{:S(2)}) async-start(), calls=%async_computation.1 | async-start | bytes 3133440 | tf_op jit(solution)/shard_map/all_gather | solution.py:219
  18.6 1.1 copy-start.7
  18.7 1.1 copy-start.8
  39.1 15.4 %copy-start.4 = (f32[16,384]{1,0:T(8,128)S(1)}, f32[16,384]{1,0:T(8,128)}, u32[]{:S(2)}) copy-start(f32[16,384]{1,0:T(8,128)} %refs_0_.1) | copy-start | bytes 73732
  39.1 15.4 %copy-start.6 = (s32[16]{0:T(128)S(1)}, s32[16]{0:T(128)}, u32[]{:S(2)}) copy-start(s32[16]{0:T(128)} %param.21) | copy-start | bytes 196
  48.0 8.1 %copy-start.10 = (s32[16]{0:T(128)S(1)}, s32[16]{0:T(128)}, u32[]{:S(2)}) copy-start(s32[16]{0:T(128)} %param.23) | copy-start | bytes 196
  127.9 4.2 %copy-start = (bf16[16,25,2304]{2,1,0:T(8,128)(2,1)S(1)}, bf16[16,25,2304]{2,1,0:T(8,128)(2,1)}, u32[]{:S(2)}) copy-start(bf16[16,25,2304]{2,1,0:T(8,128)(2,1)} %shard_map.133) | copy-start | bytes 5529604
  139.7 4.0 %copy-start.1 = (bf16[16,33,2304]{2,1,0:T(8,128)(2,1)S(1)}, bf16[16,33,2304]{2,1,0:T(8,128)(2,1)}, u32[]{:S(2)}) copy-start(bf16[16,33,2304]{2,1,0:T(8,128)(2,1)} %all-gather.7.cloned.1.call-done) | copy-start | bytes 7299076
  139.7 4.1 %copy-start.2 = (f32[256,2304]{1,0:T(8,128)S(1)}, f32[256,2304]{1,0:T(8,128)}, u32[]{:S(2)}) copy-start(f32[256,2304]{1,0:T(8,128)} %convolution_bitcast_fusion.1) | copy-start | bytes 7077892
Sparse Core Ops, SparseCore 0:
  13.0 45.4 all-gather.4
  60.7 70.1 all-gather.6

commit v9 on v7

--- a/solution.py
+++ b/solution.py
@@ -231,7 +231,9 @@
             preferred_element_type=jnp.float32,
         )
         faces.append(from_inner + from_cross)
-    face = jnp.concatenate(faces, axis=1)
+    face = jnp.zeros((group_elems, 3 * square), jnp.float32)
+    for slot in range(3):
+        face = face.at[:, slot * square : (slot + 1) * square].set(faces[slot])
 
     coarse_diag = diag_all[:, :elem_count, :].reshape(-1, square).astype(jnp.float32)
     coarse_face = face.reshape(group_width * elem_count, 3 * square)

time: 140 us -> 141 us (level)
  local copies, waits for them, and re-layouts: 7.49 us -> 10.9 us
  other arithmetic: 23.2 us -> 21.2 us
    concatenate x1 -> x0, other arithmetic: 3.21 us -> none  [per_device(): face = jnp.concatenate(faces, axis=1)]
    unnamed x28 -> x30, local copies, waits for them, and re-layouts: 1 us -> 3.94 us
    another operation x5 -> x7, other arithmetic: 2.66 us -> 3.98 us
  transfers between devices with their start and end apart: 2 -> 2, of which waited for: 1 -> 1; matrix products, arithmetic and copies ran while one was open for 28% -> 29% of each run, Pallas kernels for 43% -> 43%
where the time goes in v9:
time: 141 us
  Pallas kernels  60.1 us (43%)
  matrix products  27.6 us (20%)
  other arithmetic  21.2 us (15%)
  between operations  14.5 us (10%)
  local copies, waits for them, and re-layouts  10.9 us (8%)
  waiting for transfers between devices  6.16 us (4%)
    pallas_call x3, Pallas kernels, direct_gather(): pl.pallas_call(kernel, out_shape=tuple((jax.ShapeDtypeStruct((n,) + x.sha...  60.1 us
    dot_general x3, matrix products, coarse_terms(): jnp.einsum('rci,rdi->rcd', row_side, products, preferred_element_type=jnp...  17.4 us
    all_gather x1, waiting for transfers between devices, per_device(): face_all = lax.all_gather(face_packet, 'dom', axis=0)  6.11 us
    dot_general x3, matrix products, per_device(): jnp.einsum('sdr,drq->sq', (wanted == inner_got[None]).astype(jnp.bfloat16...  4.94 us
    another operation x7, other arithmetic  3.98 us
    unnamed x30, local copies, waits for them, and re-layouts  3.94 us
    mul x2, other arithmetic, restrictor(): full = weights[:, None, :] * table[None]  3.1 us
    convert_element_type x1, other arithmetic, per_device(): diag_all[:, :elem_count, :].reshape(-1, square).astype(jnp.float32)  2.87 us
  transfers between devices with their start and end apart: 2, of which 1 were waited for; matrix products, arithmetic and copies ran while one was open for 29% of the time, Pallas kernels for 43%

profile of v9, /device:TPU:1, one launch (start us, length us, event | category | flops | bytes accessed | tf_op | source)
XLA Modules:
  0.0 140.5 jit_solution(12938092558371576955)
XLA Ops:
  7.8 4.3 %fusion.31 = bf16[16,48,48]{2,1,0:T(8,128)(2,1)S(1)} fusion(bf16[16,384,384]{2,1,0:T(8,128)(2,1)} %param.22, f32[48,384]{1,0:T(8,128)S(1)} %mul.211, f32[16,384]{1,0:T(8,128)} %refs_0_.1), kind=kOutput, calls=%fused_computation.41 | convolution fusion | flops 256315392 | bytes 4890624 | tf_op jit(solution)/shard_map/rci,rdi->rcd/dot_general | solution.py:49
  12.1 0.8 convert_element_type.139
  13.0 0.6 compare_reduce_fusion.2
  13.7 0.6 compare_reduce_fusion.1
  14.6 0.6 fusion.72
  15.3 0.6 broadcast_select_fusion
  16.1 0.6 pad_maximum_fusion.refs_1_
  16.7 14.8 %shard_map.131 = (f32[16,16,384]{2,1,0:T(8,128)}, f32[8,16,512]{2,1,0:T(8,128)}) custom-call(f32[16,384]{1,0:T(8,128)} %refs_0_.1, f32[16,512]{1,0:T(8,128)} %pad_maximum_fusion.refs_1_), custom_call_target="tpu_custom_call" | custom-call | tf_op jit(solution)/shard_map/pallas_call | solution.py:112
  31.5 1.1 convert_reduce_fusion
  32.7 1.1 fusion.59
  33.9 0.2 fusion.87
  34.1 0.2 select_reduce_fusion
  35.2 0.4 fusion.62
  35.6 1.9 %broadcast_multiply_fusion = bf16[32,48,6,4,4,4]{1,0,5,4,3,2:T(8,128)(2,1)S(1)} fusion(f32[48,6,4,4,4]{0,4,3,2,1:T(4,128)S(1)} %broadcast_multiply_fusion.2, f32[32,6,4,4,4]{0,4,3,2,1:T(4,128)S(1)} %bitcast.72), kind=kLoop, calls=%fused_computation.24 | loop fusion | flops 1179648 | bytes 1302528 | tf_op jit(solution)/shard_map/mul | solution.py:21
  37.6 0.3 fusion.60
  37.9 1.3 reverse_select_fusion.2
  39.2 1.5 %reverse_select_fusion.1 = bf16[32,48,6,4,4,4]{1,0,5,4,3,2:T(8,128)(2,1)S(1)} fusion(bf16[32,48,6,4,4,4]{1,0,5,4,3,2:T(8,128)(2,1)S(1)} %reverse_select_fusion.2, pred[32]{0:T(512)(128)(4,1)S(1)} %get-tuple-element.71), kind=kLoop, calls=%fused_computation.1 | loop fusion | flops 589824 | bytes 2359328 | tf_op jit(solution)/shard_map/jit(_where)/select_n | solution.py:25
  40.7 1.1 fusion
  41.9 8.9 %fusion.22 = bf16[32,48,48]{2,1,0:T(8,128)(2,1)} fusion(bf16[32,384,384]{2,1,0:T(8,128)(2,1)} %param.23, bf16[32,48,384]{1,0,2:T(8,128)(2,1)S(1)} %bitcast.70, f32[48,384]{1,0:T(8,128)S(1)} %mul.211, f32[32,384]{1,0:T(8,128)S(1)} %fusion.60), kind=kOutput, calls=%fused_computation.33 | convolution fusion | flops 511451136 | bytes 10887168 | tf_op jit(solution)/shard_map/rci,rdi->rcd/dot_general | solution.py:49
  50.7 1.4 convert_element_type.149
  52.1 0.7 maximum_bitcast_fusion
  52.8 0.9 slice.112
  53.8 0.4 fusion.66
  54.2 0.2 fusion.65
  54.4 1.2 broadcast_multiply_fusion.1
  55.6 0.6 reverse_select_fusion.5
  56.2 0.7 reverse_select_fusion.4
  56.9 0.7 fusion.8
  57.6 4.3 %fusion.32 = bf16[16,48,48]{2,1,0:T(8,128)(2,1)S(1)} fusion(bf16[16,384,384]{2,1,0:T(8,128)(2,1)} %param.24, bf16[16,48,384]{1,0,2:T(8,128)(2,1)S(1)} %bitcast.71, f32[16,384]{1,0:T(8,128)S(1)} %fusion.65, f32[48,384]{1,0:T(8,128)S(1)} %mul.211), kind=kOutput, calls=%fused_computation.42 | convolution fusion | flops 255725568 | bytes 5480448 | tf_op jit(solution)/shard_map/rci,rdi->rcd/dot_general | solution.py:49
  61.8 0.8 convert_element_type.162.refs_0_
  62.7 11.9 %shard_map.132 = bf16[8,16,2304]{2,1,0:T(8,128)(2,1)} custom-call(bf16[16,2304]{1,0:T(8,128)(2,1)} %convert_element_type.162.refs_0_), custom_call_target="tpu_custom_call" | custom-call | tf_op jit(solution)/shard_map/pallas_call | solution.py:112
  74.6 1.3 convolution_convert_fusion
  75.9 0.7 reshape.665.refs_0_
  76.6 33.4 %shard_map.133 = bf16[16,24,2304]{2,1,0:T(8,128)(2,1)} custom-call(bf16[24,2304]{1,0:T(8,128)(2,1)} %reshape.665.refs_0_), custom_call_target="tpu_custom_call" | custom-call | tf_op jit(solution)/shard_map/pallas_call | solution.py:112
  110.1 0.6 compare_reduce_fusion.3
  110.7 0.7 compare_reduce_fusion
  111.4 2.9 %bitcast_convert_fusion = f32[256,2304]{1,0:T(8,128)} fusion(bf16[16,16,2304]{2,1,0:T(8,128)(2,1)} %all-gather.5.cloned.1.call-done), kind=kLoop, calls=%fused_computation.36 | loop fusion | flops 589824 | bytes 3538944 | tf_op jit(solution)/shard_map/convert_element_type | solution.py:238
  114.3 6.1 %all-gather.7.cloned.1.call-done = bf16[16,33,2304]{2,1,0:T(8,128)(2,1)} async-done(((bf16[1,33,2304]{2,1,0:T(8,128)(2,1)}), bf16[16,33,2304]{2,1,0:T(8,128)(2,1)}) %all-gather.7.cloned.1.call-update) | async-done | bytes 2433040 | tf_op jit(solution)/shard_map/all_gather | solution.py:214
  120.4 0.8 slice_convert_fusion
  121.6 0.9 convolution_bitcast_fusion.1
  122.6 0.9 convolution_bitcast_fusion.2
  123.5 0.9 copy-done.1
  124.4 1.9 %fusion.2 = f32[256,2304]{1,0:T(8,128)S(1)} fusion(f32[256,2304]{1,0:T(8,128)S(1)} %convolution_bitcast_fusion.2, bf16[16,33,2304]{2,1,0:T(8,128)(2,1)S(1)} %copy-done.1, pred[]{:T(512)} %compare_reduce_fusion.3, s32[16,33]{1,0:T(8,128)S(1)} %slice_select_fusion, s32[256]{0:T(256)S(1)} %iota_multiply_fusion), kind=kOutput, calls=%fused_computation.14 | convolution fusion | flops 624168960 | bytes 7154753 | tf_op jit(solution)/shard_map/sdr,drq->sq/dot_general | solution.py:225
  126.3 0.5 scatter.20
  126.7 0.9 convolution_bitcast_fusion
  127.6 1.8 %fusion.5 = f32[256,6912]{1,0:T(8,128)S(1)} fusion(f32[256,6912]{1,0:T(8,128)S(1)} %scatter.20, f32[256,2304]{1,0:T(8,128)S(1)} %convolution_bitcast_fusion.1, bf16[16,33,2304]{2,1,0:T(8,128)(2,1)S(1)} %copy-done.1, pred[]{:T(512)} %compare_reduce_fusion, s32[256]{0:T(256)S(1)} %fusion.71, s32[16,33]{1,0:T(8,128)S(1)} %slice_select_fusion), kind=kOutput, calls=%fused_computation.17 | convolution fusion | flops 624168960 | bytes 7676929 | tf_op jit(solution)/shard_map/sdr,drq->sq/dot_general | solution.py:225
  129.5 1.3 fusion.7
  130.7 3.0 %copy-done.2 = f32[256,6912]{1,0:T(8,128)} copy-done((f32[256,6912]{1,0:T(8,128)}, f32[256,6912]{1,0:T(8,128)S(1)}, u32[]{:S(2)}) %copy-start.2) | copy-done | bytes 7077912
  (76 shorter events, 2.6 us)
Async XLA Ops:
  7.2 104.3 %all-gather.5.cloned.1.call-start = ((), (), s32[]{:S(2)}) async-start(), calls=%async_computation | async-start | bytes 1253376 | tf_op jit(solution)/shard_map/all_gather | solution.py:193
  7.7 6.8 %copy-start.13 = (s32[16,1]{0,1:T(1,128)S(1)}, s32[16,1]{0,1:T(1,128)}, u32[]{:S(2)}) copy-start(s32[16,1]{0,1:T(1,128)} %param.31) | copy-start | bytes 196
  7.7 6.9 %copy-start.14 = (s32[16]{0:T(128)S(1)}, s32[16]{0:T(128)}, u32[]{:S(2)}) copy-start(s32[16]{0:T(128)} %param.33) | copy-start | bytes 196
  7.7 8.4 %copy-start.3 = (f32[16,384]{1,0:T(8,128)S(1)}, f32[16,384]{1,0:T(8,128)}, u32[]{:S(2)}) copy-start(f32[16,384]{1,0:T(8,128)} %refs_0_.1) | copy-start | bytes 73732
  7.7 26.7 %copy-start.9 = (s32[32]{0:T(128)S(1)}, s32[32]{0:T(128)}, u32[]{:S(2)}) copy-start(s32[32]{0:T(128)} %param.32) | copy-start | bytes 388
  7.8 26.7 %copy-start.10 = (s32[32,1]{0,1:T(1,128)S(1)}, s32[32,1]{0,1:T(1,128)}, u32[]{:S(2)}) copy-start(s32[32,1]{0,1:T(1,128)} %param.30) | copy-start | bytes 388
  7.8 27.4 %copy-start.4 = (f32[16,384]{1,0:T(8,128)S(1)}, f32[16,384]{1,0:T(8,128)}, u32[]{:S(2)}) copy-start(f32[16,384]{1,0:T(8,128)} %refs_0_.1) | copy-start | bytes 73732
  7.8 27.4 %copy-start.6 = (s32[32]{0:T(128)S(1)}, s32[32]{0:T(128)}, u32[]{:S(2)}) copy-start(s32[32]{0:T(128)} %param.26) | copy-start | bytes 388
  7.8 27.8 %copy-start.11 = (s32[32]{0:T(128)S(1)}, s32[32]{0:T(128)}, u32[]{:S(2)}) copy-start(s32[32]{0:T(128)} %param.28) | copy-start | bytes 388
  13.0 107.4 %all-gather.7.cloned.1.call-start = ((), (), s32[]{:S(2)}) async-start(), calls=%async_computation.1 | async-start | bytes 3133440 | tf_op jit(solution)/shard_map/all_gather | solution.py:214
  34.4 3.2 %copy-start.5 = (f32[16,16,384]{2,1,0:T(8,128)S(1)}, f32[16,16,384]{2,1,0:T(8,128)}, u32[]{:S(2)}) copy-start(f32[16,16,384]{2,1,0:T(8,128)} %get-tuple-element.64) | copy-start | bytes 1179652
  41.8 12.0 %copy-start.12 = (s32[16]{0:T(128)S(1)}, s32[16]{0:T(128)}, u32[]{:S(2)}) copy-start(s32[16]{0:T(128)} %param.29) | copy-start | bytes 196
  41.8 12.0 %copy-start.7 = (s32[16]{0:T(128)S(1)}, s32[16]{0:T(128)}, u32[]{:S(2)}) copy-start(s32[16]{0:T(128)} %param.27) | copy-start | bytes 196
  110.0 11.6 %copy-start = (bf16[16,24,2304]{2,1,0:T(8,128)(2,1)S(1)}, bf16[16,24,2304]{2,1,0:T(8,128)(2,1)}, u32[]{:S(2)}) copy-start(bf16[16,24,2304]{2,1,0:T(8,128)(2,1)} %shard_map.133) | copy-start | bytes 5308420
  122.5 0.9 copy-start.8
  122.5 1.8 %copy-start.1 = (bf16[16,33,2304]{2,1,0:T(8,128)(2,1)S(1)}, bf16[16,33,2304]{2,1,0:T(8,128)(2,1)}, u32[]{:S(2)}) copy-start(bf16[16,33,2304]{2,1,0:T(8,128)(2,1)} %all-gather.7.cloned.1.call-done) | copy-start | bytes 7299076
  130.7 3.0 %copy-start.2 = (f32[256,6912]{1,0:T(8,128)}, f32[256,6912]{1,0:T(8,128)S(1)}, u32[]{:S(2)}) copy-start(f32[256,6912]{1,0:T(8,128)S(1)} %fusion.7) | copy-start | bytes 21233668
Sparse Core Ops, SparseCore 0:
  13.1 44.5 all-gather.4
  60.4 59.9 all-gather.6
